TPU v7x, 128 devices: a whole 4x4x4 slice. The times are simulated.
128 devices in a mesh: seq: 16 (over x, y), grp: 8 (over z, core).
Axes of the slice: x: 4, y: 4, z: 4, core: 2. Of those that a mesh axis runs over, the one named last changes fastest.
Arguments:
- tokens: bfloat16 [8, 16384, 3072], P('grp', 'seq'), may hold values from -24 to 24
- block_map: int32 [8, 128], P('grp', 'seq'), may hold values from 0 to 1, as said below
- slot_keys: bfloat16 [3072, 256], replicated, may hold values from -2 to 2
- gate_weight: bfloat16 [16, 3072, 4096], P('grp', None, 'seq'), may hold values from -0.109375 to 0.109375
- up_weight: bfloat16 [16, 3072, 4096], P('grp', None, 'seq'), may hold values from -0.109375 to 0.109375
- down_weight: bfloat16 [16, 4096, 3072], P('grp', 'seq'), may hold values from -0.09375 to 0.09375
Outputs:
- mixed: bfloat16 [8, 16384, 3072], P('grp', 'seq')
Inputs may be any that keep to these rules, and one draw needn't show every extreme that they name: `block_map`: every sequence has at least one image block and at least one text block.
All inputs are finite; a program needn't handle non-finite values.
Results may differ from a plain program's by a relative error of at most 0.014.
Values may be sent and summed in bfloat16 or wider, within the bound.
A program may use at most 128 MiB of HBM per device.

v0:
```python
import jax
import jax.numpy as jnp
from jax import lax
from jax.sharding import PartitionSpec as P

BLOCK = 128


def sent_to_all(shard, axis):
    copies = jnp.broadcast_to(shard, (lax.axis_size(axis), *shard.shape))
    return lax.all_to_all(copies, axis, split_axis=0, concat_axis=0, tiled=True)


def taken_together(shard, axis):
    return sent_to_all(shard, axis).max(axis=0)


def in_blocks(shard, dim, peers):
    shape = shard.shape
    parts = shard.reshape(*shape[:dim], peers, shape[dim] // peers, *shape[dim + 1 :])
    return jnp.moveaxis(parts, dim, 0)


def summed_on_arrival(shard, axis, dim):
    peers = lax.axis_size(axis)
    parts = lax.all_to_all(in_blocks(shard, dim, peers), axis, 0, 0, tiled=True)
    return jnp.sum(parts, axis=0)


def taken_together_2(shard, axis):
    return sent_to_all(shard, axis).sum(axis=0)


def laid_out(parts, dim):
    parts = jnp.moveaxis(parts, 0, dim)
    shape = parts.shape
    return parts.reshape(*shape[:dim], shape[dim] * shape[dim + 1], *shape[dim + 2 :])


def gather_directly(shard, axis, dim):
    parts = sent_to_all(shard, axis)
    return laid_out(parts, dim)


def body(tokens, block_map, slot_keys, gate_weight, up_weight, down_weight):
    seq_tokens = tokens[0]
    rows_here = seq_tokens.shape[0]
    slot_count = slot_keys.shape[1]
    groups = lax.axis_size("grp")
    exp_dev = gate_weight.shape[0]
    per_expert = slot_count // (groups * exp_dev)
    image_slots = 3 * slot_count // 4
    slot_text = (jnp.arange(slot_count) >= image_slots).astype(jnp.int32)
    block_total = block_map.shape[1]
    allowed = block_map[0][:, None, None] == slot_text[None, None, :]
    allowed = jnp.broadcast_to(allowed, (block_total, BLOCK, slot_count)).reshape(
        rows_here, slot_count
    )
    logits = jnp.dot(seq_tokens, slot_keys, preferred_element_type=jnp.float32)
    masked = jnp.where(allowed, logits, -1e30)
    local_peak = jnp.max(masked, axis=0)
    global_peak = taken_together(local_peak, "seq")
    weights = jnp.where(allowed, jnp.exp(masked - global_peak[None, :]), 0.0)
    totals_loc = jnp.sum(weights, axis=0)
    rows_loc = jnp.einsum(
        "ts,td->sd", weights.astype(jnp.bfloat16), seq_tokens, preferred_element_type=jnp.float32
    )
    totals_loc, rows_loc = (totals_loc, rows_loc)
    rows_part = summed_on_arrival(rows_loc, "seq", 1)
    totals = taken_together_2(totals_loc, "seq")
    slot_part = (rows_part / totals[:, None]).astype(jnp.bfloat16)
    col_width = slot_part.shape[1]
    arrived = lax.all_to_all(
        slot_part.reshape(groups, slot_count // groups, col_width),
        "grp",
        split_axis=0,
        concat_axis=0,
        tiled=True,
    )
    arrived = arrived.reshape(groups, exp_dev, per_expert, col_width)
    columns_in = gather_directly(arrived, "seq", 3)
    gate_more = jnp.einsum(
        "gesd,edf->gesf", columns_in, gate_weight, preferred_element_type=jnp.float32
    )
    up_more = jnp.einsum(
        "gesd,edf->gesf", columns_in, up_weight, preferred_element_type=jnp.float32
    )
    hidden = (jax.nn.silu(gate_more) * up_more).astype(jnp.bfloat16)
    partial_value = jnp.einsum(
        "gesf,efd->gesd", hidden, down_weight, preferred_element_type=jnp.float32
    )
    owned_part = summed_on_arrival(partial_value, "seq", 3).astype(jnp.bfloat16)
    returned = lax.all_to_all(owned_part, "grp", split_axis=0, concat_axis=0, tiled=True)
    row_peak = jnp.max(masked, axis=1)
    scores = jnp.where(allowed, jnp.exp(masked - row_peak[:, None]), 0.0)
    mix_weights = (scores / jnp.sum(scores, axis=1)[:, None]).astype(jnp.bfloat16)
    columns_in = gather_directly(returned, "seq", 3)
    flat_slots = columns_in.reshape(slot_count, columns_in.shape[3])
    output = jnp.dot(mix_weights, flat_slots, preferred_element_type=jnp.float32)
    return output.astype(jnp.bfloat16)[None]


def solution(mesh):
    placed = (
        P("grp", "seq", None),
        P("grp", "seq"),
        P(),
        P("grp", None, "seq"),
        P("grp", None, "seq"),
        P("grp", "seq", None),
    )
    return jax.shard_map(
        body, mesh=mesh, in_specs=placed, out_specs=P("grp", "seq", None), check_vma=False
    )
```

profile of v0, /device:TPU:0, one launch (start us, length us, event | category | flops | bytes accessed | tf_op | source)
XLA Modules:
  0.0 274.9 jit_solution(6317611544944362076)
XLA Ops:
  0.0 0.0 copy-start
  0.0 0.9 broadcast_compare_fusion
  0.9 6.1 %fusion.28 = (f32[256]{0:T(256)S(1)}, f32[1024]{0:T(1024)S(1)}, f32[1024,256]{1,0:T(8,128)}) fusion(bf16[3072,256]{1,0:T(8,128)(2,1)} %param.8, bf16[1,1024,3072]{2,1,0:T(8,128)(2,1)} %param.6, pred[8,256]{1,0:T(8,128)(4,1)S(1)} %broadcast_compare_fusion), kind=kOutput, calls=%fused_computation.27 | convolution fusion | flops 1611397888 | bytes 8920064 | tf_op jit(solution)/shard_map/dot_general | solution.py:59
  7.0 0.6 broadcast_in_dim.36
  7.6 7.1 %all-to-all-start = ((f32[16,1,256]{2,1,0:T(1,128)}), f32[16,1,256]{2,1,0:T(1,128)S(1)}, u32[]{:S(2)}, u32[]{:S(2)}) async-start(f32[16,1,256]{2,1,0:T(1,128)} %broadcast_in_dim.36), calls=%async_computation | async-start | bytes 32768 | tf_op jit(solution)/shard_map/all_to_all | solution.py:11
  14.7 8.6 %copy.42 = bf16[1,1024,3072]{1,2,0:T(8,128)(2,1)} copy(bf16[1,1024,3072]{2,1,0:T(8,128)(2,1)} %param.6) | data formatting | bytes 12582912 | tf_op args[0]
  23.3 0.0 all-to-all-done
  23.4 2.4 fusion.22
  25.7 0.6 broadcast_in_dim.37
  26.3 7.2 %all-to-all-start.2 = ((f32[16,1,256]{2,1,0:T(1,128)}), f32[16,1,256]{2,1,0:T(1,128)S(1)}, u32[]{:S(2)}, u32[]{:S(2)}) async-start(f32[16,1,256]{2,1,0:T(1,128)} %broadcast_in_dim.37), calls=%async_computation.2 | async-start | bytes 32768 | tf_op jit(solution)/shard_map/all_to_all | solution.py:11
  33.6 6.4 %convolution_bitcast_fusion.1 = f32[16,256,192]{1,2,0:T(8,128)} fusion(bf16[16,192,1024]{2,1,0:T(8,128)(2,1)} %bitcast.95, bf16[1024,256]{1,0:T(8,128)(2,1)} %get-tuple-element.9), kind=kOutput, calls=%fused_computation.13 | convolution fusion | flops 1610612736 | bytes 9961472 | tf_op jit(solution)/shard_map/ts,td->sd/dot_general | solution.py:65
  40.0 1.2 all-to-all-done.2
  41.2 6.1 %all-to-all-start.1 = ((f32[16,256,192]{1,2,0:T(8,128)}), f32[16,256,192]{1,2,0:T(8,128)}, u32[]{:S(2)}, u32[]{:S(2)}) async-start(f32[16,256,192]{1,2,0:T(8,128)} %convolution_bitcast_fusion.1), calls=%async_computation.1 | async-start | bytes 6291456 | tf_op jit(solution)/shard_map/all_to_all | solution.py:26
  47.3 0.1 div.25
  47.4 41.4 %all-to-all-done.1 = f32[16,256,192]{1,2,0:T(8,128)} async-done(((f32[16,256,192]{1,2,0:T(8,128)}), f32[16,256,192]{1,2,0:T(8,128)}, u32[]{:S(2)}, u32[]{:S(2)}) %all-to-all-start.1) | async-done | bytes 3145760 | tf_op jit(solution)/shard_map/all_to_all | solution.py:26
  88.8 2.8 %reduce_sum.48 = f32[256,192]{0,1:T(8,128)} reduce(f32[16,256,192]{1,2,0:T(8,128)} %all-to-all-done.1, f32[]{:T(128)} %constant.4.clone.1), dimensions={0}, to_apply=%region_4.5 | reduce | flops 737280 | bytes 3342340 | tf_op jit(solution)/shard_map/reduce_sum | solution.py:27
  91.6 1.1 copy.44
  92.7 0.1 divide_convert_fusion.1
  92.8 11.3 %all_to_all.42 = bf16[8,32,192]{2,1,0:T(8,128)(2,1)S(1)} all-to-all(bf16[8,32,192]{2,1,0:T(8,128)(2,1)S(1)} %divide_convert_fusion.1), channel_id=1, replica_groups=mesh['seq'=16,'grp'=8] {'grp'}, dimensions={0} | all-to-all | bytes 196608 | tf_op jit(solution)/shard_map/all_to_all | solution.py:73
  104.1 0.2 broadcast_in_dim.38
  104.3 31.9 %all_to_all.43 = bf16[16,8,2,16,192]{4,3,1,2,0:T(8,128)(2,1)S(1)} all-to-all(bf16[16,8,2,16,192]{4,3,1,2,0:T(8,128)(2,1)S(1)} %broadcast_in_dim.38), channel_id=1, replica_groups=mesh['seq'=16,'grp'=8] {'seq'}, dimensions={0} | all-to-all | bytes 3145728 | tf_op jit(solution)/shard_map/all_to_all | solution.py:11
  136.2 2.5 copy.47
  138.7 4.5 %reshape.72 = bf16[8,2,16,3072]{3,2,0,1:T(8,128)(2,1)} reshape(bf16[8,2,16,16,192]{4,3,2,0,1:T(8,128)(2,1)} %copy.47) | data formatting | bytes 3145728 | tf_op jit(solution)/shard_map/reshape | solution.py:37
  143.2 2.9 %fusion.9 = f32[8,2,16,256]{3,2,0,1:T(8,128)S(1)} fusion(bf16[8,2,16,3072]{3,2,0,1:T(8,128)(2,1)} %reshape.72, bf16[2,3072,256]{2,1,0:T(8,128)(2,1)} %param.9), kind=kOutput, calls=%fused_computation.14 | convolution fusion | flops 402653184 | bytes 4980736 | tf_op jit(solution)/shard_map/gesd,edf->gesf/dot_general | solution.py:82
  146.2 0.0 copy-done
  146.2 5.1 %convolution_bitcast_fusion = f32[8,2,16,3072]{3,2,0,1:T(8,128)} fusion(bf16[2,256,3072]{2,1,0:T(8,128)(2,1)S(1)} %copy-done, bf16[8,2,16,3072]{3,2,0,1:T(8,128)(2,1)} %reshape.72, bf16[2,3072,256]{2,1,0:T(8,128)(2,1)} %param.10, f32[8,2,16,256]{3,2,0,1:T(8,128)S(1)} %fusion.9), kind=kOutput, calls=%fused_computation.4 | convolution fusion | flops 805699584 | bytes 11272192 | tf_op jit(solution)/shard_map/gesf,efd->gesd/dot_general | solution.py:89
  151.3 5.5 %reshape.73 = f32[8,2,16,16,192]{4,3,2,0,1:T(8,128)} reshape(f32[8,2,16,3072]{3,2,0,1:T(8,128)} %convolution_bitcast_fusion) | data formatting | bytes 6291456 | tf_op jit(solution)/shard_map/reshape | solution.py:20
  156.8 4.6 %copy.59 = f32[8,2,16,16,192]{4,2,0,1,3:T(8,128)S(1)} copy(f32[8,2,16,16,192]{4,3,2,0,1:T(8,128)} %reshape.73) | data formatting | bytes 6291456 | tf_op jit(solution)/shard_map/reshape | solution.py:20
  161.4 52.8 %all_to_all.44 = f32[16,8,2,16,192]{4,3,1,2,0:T(8,128)} all-to-all(f32[16,8,2,16,192]{4,3,1,2,0:T(8,128)S(1)} %bitcast.92), channel_id=1, replica_groups=mesh['seq'=16,'grp'=8] {'seq'}, dimensions={0} | all-to-all | bytes 6291456 | tf_op jit(solution)/shard_map/all_to_all | solution.py:26
  214.2 2.7 reduce_sum.52
  216.9 8.8 %all_to_all.45 = bf16[8,2,16,192]{3,2,1,0:T(8,128)(2,1)S(1)} all-to-all(bf16[8,2,16,192]{3,2,1,0:T(8,128)(2,1)S(1)} %copy.50), channel_id=1, replica_groups=mesh['seq'=16,'grp'=8] {'grp'}, dimensions={0} | all-to-all | bytes 196608 | tf_op jit(solution)/shard_map/all_to_all | solution.py:93
  225.7 0.0 copy-start.2
  225.7 1.6 broadcast_in_dim.39
  227.3 4.3 %all-to-all-start.7 = ((bf16[16,8,2,16,192]{4,3,2,1,0:T(8,128)(2,1)}), bf16[16,8,2,16,192]{4,3,2,1,0:T(8,128)(2,1)S(1)}, u32[]{:S(2)}, u32[]{:S(2)}) async-start(bf16[16,8,2,16,192]{4,3,2,1,0:T(8,128)(2,1)} %broadcast_in_dim.39), calls=%async_computation.7 | async-start | bytes 4194304 | tf_op jit(solution)/shard_map/all_to_all | solution.py:11
  231.6 0.0 copy-done.2
  231.6 1.2 divide_convert_fusion
  232.8 28.8 %all-to-all-done.7 = bf16[16,8,2,16,192]{4,3,2,1,0:T(8,128)(2,1)S(1)} async-done(((bf16[16,8,2,16,192]{4,3,2,1,0:T(8,128)(2,1)}), bf16[16,8,2,16,192]{4,3,2,1,0:T(8,128)(2,1)S(1)}, u32[]{:S(2)}, u32[]{:S(2)}) %all-to-all-start.7) | async-done | bytes 1572896 | tf_op jit(solution)/shard_map/all_to_all | solution.py:11
  261.6 2.6 copy.51
  264.2 0.0 copy-start.1
  264.2 4.7 %reshape_reshape.3 = bf16[256,3072]{1,0:T(8,128)(2,1)} reshape(bf16[8,2,16,16,192]{4,3,2,1,0:T(8,128)(2,1)} %copy.51) | data formatting | bytes 3145728 | tf_op jit(solution)/shard_map/reshape;reshape | solution.py:98
  268.8 6.1 %convert_bitcast_fusion = bf16[1,1024,3072]{2,1,0:T(8,128)(2,1)} fusion(bf16[1024,256]{1,0:T(8,128)(2,1)} %divide_convert_fusion, bf16[256,3072]{1,0:T(8,128)(2,1)} %reshape_reshape.3), kind=kOutput, calls=%fused_computation.2 | convolution fusion | flops 1613758464 | bytes 8388608 | tf_op jit(solution)/shard_map/dot_general | solution.py:99
  274.9 0.0 copy-done.1
  (5 shorter events, 0.1 us)
Async XLA Ops:
  0.0 146.2 %copy-start = (bf16[2,256,3072]{2,1,0:T(8,128)(2,1)S(1)}, bf16[2,256,3072]{2,1,0:T(8,128)(2,1)}, u32[]{:S(2)}) copy-start(bf16[2,256,3072]{2,1,0:T(8,128)(2,1)} %param.11) | copy-start | bytes 9437188
  7.6 15.7 %all-to-all-start = ((f32[16,1,256]{2,1,0:T(1,128)}), f32[16,1,256]{2,1,0:T(1,128)S(1)}, u32[]{:S(2)}, u32[]{:S(2)}) async-start(f32[16,1,256]{2,1,0:T(1,128)} %broadcast_in_dim.36), calls=%async_computation | async-start | bytes 32768 | tf_op jit(solution)/shard_map/all_to_all | solution.py:11
  26.3 14.8 %all-to-all-start.2 = ((f32[16,1,256]{2,1,0:T(1,128)}), f32[16,1,256]{2,1,0:T(1,128)S(1)}, u32[]{:S(2)}, u32[]{:S(2)}) async-start(f32[16,1,256]{2,1,0:T(1,128)} %broadcast_in_dim.37), calls=%async_computation.2 | async-start | bytes 32768 | tf_op jit(solution)/shard_map/all_to_all | solution.py:11
  41.2 47.7 %all-to-all-start.1 = ((f32[16,256,192]{1,2,0:T(8,128)}), f32[16,256,192]{1,2,0:T(8,128)}, u32[]{:S(2)}, u32[]{:S(2)}) async-start(f32[16,256,192]{1,2,0:T(8,128)} %convolution_bitcast_fusion.1), calls=%async_computation.1 | async-start | bytes 6291456 | tf_op jit(solution)/shard_map/all_to_all | solution.py:26
  225.7 5.9 %copy-start.2 = (f32[1024,256]{1,0:T(8,128)S(1)}, f32[1024,256]{1,0:T(8,128)}, u32[]{:S(2)}) copy-start(f32[1024,256]{1,0:T(8,128)} %get-tuple-element.10) | copy-start | bytes 3145732
  227.3 34.3 %all-to-all-start.7 = ((bf16[16,8,2,16,192]{4,3,2,1,0:T(8,128)(2,1)}), bf16[16,8,2,16,192]{4,3,2,1,0:T(8,128)(2,1)S(1)}, u32[]{:S(2)}, u32[]{:S(2)}) async-start(bf16[16,8,2,16,192]{4,3,2,1,0:T(8,128)(2,1)} %broadcast_in_dim.39), calls=%async_computation.7 | async-start | bytes 4194304 | tf_op jit(solution)/shard_map/all_to_all | solution.py:11
  264.2 10.7 %copy-start.1 = (bf16[2,256,3072]{2,1,0:T(8,128)(2,1)S(1)}, bf16[2,256,3072]{2,1,0:T(8,128)(2,1)}, u32[]{:S(2)}) copy-start(bf16[2,256,3072]{2,1,0:T(8,128)(2,1)} %param.11) | copy-start | bytes 9437188
where the time goes:
time: 276 us; the launch traced here: 275 us
  blocking collectives  105 us (38%)
  waiting for transfers between devices  71.4 us (26%)
  local copies, waits for them, and re-layouts  37.1 us (13%)
  matrix products  26.7 us (10%)
  starting transfers between devices  24.7 us (9%)
  other arithmetic  10 us (4%)
    all_to_all x1, blocking collectives, summed_on_arrival(): parts = lax.all_to_all(in_blocks(shard, dim, peers), axis, 0, 0, tiled=True)  52.8 us
    all_to_all x1, waiting for transfers between devices, summed_on_arrival(): parts = lax.all_to_all(in_blocks(shard, dim, peers), axis, 0, 0, tiled=True)  41.4 us
    all_to_all x1, blocking collectives, sent_to_all(): return lax.all_to_all(copies, axis, split_axis=0, concat_axis=0, tiled=True)  31.9 us
    all_to_all x3, waiting for transfers between devices, sent_to_all(): return lax.all_to_all(copies, axis, split_axis=0, concat_axis=0, tiled=True)  30 us
    all_to_all x3, starting transfers between devices, sent_to_all(): return lax.all_to_all(copies, axis, split_axis=0, concat_axis=0, tiled=True)  18.6 us
    all_to_all x1, blocking collectives, body(): lax.all_to_all(slot_part.reshape(groups, slot_count // groups, col_width)...  11.3 us
    reshape x2, local copies, waits for them, and re-layouts, in_blocks(): shard.reshape(*shape[:dim], peers, shape[dim] // peers, *shape[dim + 1:])  10.1 us
    all_to_all x1, blocking collectives, body(): lax.all_to_all(owned_part, 'grp', split_axis=0, concat_axis=0, tiled=True)  8.8 us
  transfers between devices with their start and end apart: 4, of which 3 were waited for; matrix products, arithmetic and copies ran while one was open for 6% of the time, Pallas kernels for 0%

commit v1 on v0

v1 whole, which is shorter than its diff:
```python
import functools
import jax
import jax.numpy as jnp
from jax import lax
from jax.experimental import pallas as pl
from jax.experimental.pallas import tpu as pltpu
from jax.sharding import PartitionSpec as P

BLOCK = 128
MESH = pl.DeviceIdType.MESH
F32 = jnp.float32
BF16 = jnp.bfloat16


def loop(start, stop, fn):
    def step(k, carry):
        fn(k)
        return carry

    lax.fori_loop(start, stop, step, 0)


def layer_kernel(
    dims,
    tok_hbm,
    bm_ref,
    keys_hbm,
    wg_hbm,
    wu_hbm,
    wd_hbm,
    mix_hbm,
    slots_hbm,
    tok,
    keys,
    wg,
    wu,
    wd,
    logits,
    wts,
    mixb,
    rows_f,
    fac,
    stat,
    sbuf_a,
    rbuf_a,
    part_b,
    recv_b,
    xin,
    sbuf_e,
    rbuf_e,
    part_f,
    recv_f,
    acc,
    tok_sem,
    in_sem,
    mix_sem,
    own_sem,
    st_s,
    st_r,
    a_s,
    a_r,
    b_s,
    b_r,
    c_s,
    c_r,
    e_s,
    e_r,
    f_s,
    f_r,
    g_s,
    g_r,
):
    nseq, ngrp, image_slots = dims
    me = lax.axis_index("seq")
    grp = lax.axis_index("grp")
    rows, width = tok.shape
    slots = keys.shape[1]
    cblocks = nseq // 2
    cw = width // cblocks
    half = me // cblocks
    col = pl.multiple_of(lax.rem(me, cblocks) * cw, cw)

    tchunk = rows // 4
    keys_copy = pltpu.make_async_copy(keys_hbm, keys, in_sem.at[0])
    keys_copy.start()

    def tok_copy(r):
        at = pl.ds(pl.multiple_of(r * tchunk, tchunk), tchunk)
        return pltpu.make_async_copy(tok_hbm.at[0, at], tok.at[at], tok_sem.at[r])

    loop(0, 4, lambda r: tok_copy(r).start())
    wg_copy = pltpu.make_async_copy(wg_hbm, wg, in_sem.at[1])
    wu_copy = pltpu.make_async_copy(wu_hbm, wu, in_sem.at[2])
    wd_copy = pltpu.make_async_copy(wd_hbm, wd, in_sem.at[3])
    wg_copy.start()
    wu_copy.start()
    wd_copy.start()

    barrier = pltpu.get_barrier_semaphore()

    def greet(axis, n, mine):
        def go(k):
            pl.semaphore_signal(
                barrier, inc=1, device_id={axis: lax.rem(mine + k, n)}, device_id_type=MESH
            )

        loop(1, n, go)

    greet("seq", nseq, me)
    greet("grp", ngrp, grp)

    def to(src, dst, ssem, rsem, axis, peer):
        return pltpu.make_async_remote_copy(
            src_ref=src,
            dst_ref=dst,
            send_sem=ssem,
            recv_sem=rsem,
            device_id={axis: peer},
            device_id_type=MESH,
        )

    text_lane = (lax.broadcasted_iota(jnp.int32, (1, slots), 1) >= image_slots).astype(jnp.int32)

    keys_copy.wait()

    per = tchunk // BLOCK

    def logit_chunk(r, peak):
        tok_copy(r).wait()
        at = pl.ds(pl.multiple_of(r * tchunk, tchunk), tchunk)
        got = jnp.dot(tok[at], keys[...], preferred_element_type=F32)
        for b in range(per):
            block = jnp.where(
                text_lane == bm_ref[0, r * per + b], got[b * BLOCK : (b + 1) * BLOCK], -1e30
            )
            logits[pl.ds(pl.multiple_of(r * tchunk + b * BLOCK, BLOCK), BLOCK)] = block
            peak = jnp.maximum(peak, jnp.max(block, axis=0, keepdims=True))
        return peak

    peak = lax.fori_loop(0, 4, logit_chunk, jnp.full((1, slots), -1e30, F32))

    def weigh(b, total):
        at = pl.ds(pl.multiple_of(b * BLOCK, BLOCK), BLOCK)
        w = jnp.where(text_lane == bm_ref[0, b], jnp.exp(logits[at] - peak), 0.0)
        wts[:, at] = w.T.astype(BF16)
        return total + jnp.sum(w, axis=0, keepdims=True)

    total = lax.fori_loop(0, rows // BLOCK, weigh, jnp.zeros((1, slots), F32))
    stat[me, 0:1] = peak
    stat[me, 1:2] = total

    pl.semaphore_wait(barrier, nseq - 1 + ngrp - 1)

    def stat_copy(k, peer, src):
        return to(stat.at[src], stat.at[src], st_s.at[k], st_r.at[src], "seq", peer)

    loop(1, nseq, lambda k: stat_copy(k, lax.rem(me + k, nseq), me).start())

    rw = 2 * cw

    def rows_block(n):
        at = pl.ds(pl.multiple_of(n * rw, rw), rw)
        rows_f[:, at] = jnp.dot(wts[...], tok[:, at], preferred_element_type=F32)

    loop(0, width // rw, rows_block)

    def stat_done(k):
        p = lax.rem(me + nseq - k, nseq)
        stat_copy(k, p, p).wait_recv()

    loop(1, nseq, stat_done)
    peaks = stat[:, 0, :]
    top = jnp.max(peaks, axis=0, keepdims=True)
    whole = jnp.sum(jnp.exp(peaks - top) * stat[:, 1, :], axis=0, keepdims=True)
    fac_row = jnp.exp(peak - top) / whole
    fac[...] = jnp.broadcast_to(fac_row, (BLOCK, slots)).T

    per_expert = 16
    groups = slots // (2 * per_expert)

    def scatter_a(k):
        d = lax.rem(me + k, nseq)
        h = d // cblocks
        at = pl.ds(pl.multiple_of(lax.rem(d, cblocks) * cw, cw), cw)
        for g in range(groups):
            src = pl.ds(pl.multiple_of((2 * g + h) * per_expert, per_expert), per_expert)
            scale = fac[src]
            scale = jnp.concatenate([scale] * (cw // BLOCK), axis=1)
            sbuf_a[d, g * per_expert : (g + 1) * per_expert] = (rows_f[src, at] * scale).astype(
                BF16
            )

    def a_copy(k, d, src):
        return to(sbuf_a.at[d], rbuf_a.at[src], a_s.at[k], a_r.at[src], "seq", d)

    def send_a(k):
        scatter_a(k)
        a_copy(k, lax.rem(me + k, nseq), me).start()

    loop(1, nseq, send_a)
    scatter_a(0)

    def mix_block(b):
        at = pl.ds(pl.multiple_of(b * BLOCK, BLOCK), BLOCK)
        m = logits[at]
        e = jnp.where(
            text_lane == bm_ref[0, b], jnp.exp(m - jnp.max(m, axis=1, keepdims=True)), 0.0
        )
        mixb[at] = (e / jnp.sum(e, axis=1, keepdims=True)).astype(BF16)

    loop(0, rows // BLOCK, mix_block)
    mix_copy = pltpu.make_async_copy(mixb, mix_hbm, mix_sem)
    mix_copy.start()

    acc[...] = sbuf_a[me].astype(F32)

    def gather_a(k):
        p = lax.rem(me + nseq - k, nseq)
        a_copy(k, p, p).wait_recv()
        acc[...] += rbuf_a[p].astype(F32)

    loop(1, nseq, gather_a)
    part_b[...] = acc[...].astype(BF16).reshape(part_b.shape)

    def b_copy(k, d, src):
        return to(part_b.at[d], recv_b.at[src], b_s.at[k], b_r.at[src], "grp", d)

    loop(1, ngrp, lambda k: b_copy(k, lax.rem(grp + k, ngrp), grp).start())
    recv_b[grp] = part_b[grp]

    def b_done(k):
        p = lax.rem(grp + ngrp - k, ngrp)
        b_copy(k, p, p).wait_recv()

    loop(1, ngrp, b_done)

    def c_copy(k, d, h, at, src):
        return to(recv_b, xin.at[h, :, :, at], c_s.at[k], c_r.at[src], "seq", d)

    loop(1, nseq, lambda k: c_copy(k, lax.rem(me + k, nseq), half, pl.ds(col, cw), me).start())
    xin[half, :, :, pl.ds(col, cw)] = recv_b[...]

    def c_done(k):
        p = lax.rem(me + nseq - k, nseq)
        at = pl.ds(pl.multiple_of(lax.rem(p, cblocks) * cw, cw), cw)
        c_copy(k, p, p // cblocks, at, p).wait_recv()

    loop(1, nseq, c_done)
    wg_copy.wait()
    wu_copy.wait()
    wd_copy.wait()

    lanes = ngrp * per_expert

    def expert(h):
        x = xin[h].reshape(lanes, width)
        gate = jnp.dot(x, wg[h], preferred_element_type=F32)
        up = jnp.dot(x, wu[h], preferred_element_type=F32)
        hidden = (gate / (1.0 + jnp.exp(-gate)) * up).astype(BF16)

        def down(c):
            at = pl.ds(pl.multiple_of(c * rw, rw), rw)
            out = jnp.dot(hidden, wd[h, :, at], preferred_element_type=F32).astype(BF16)
            sbuf_e[h * cblocks + 2 * c] = out[:, :cw]
            sbuf_e[h * cblocks + 2 * c + 1] = out[:, cw:]

        loop(0, cblocks // 2, down)

    loop(0, 2, expert)

    def e_copy(k, d, src):
        return to(sbuf_e.at[d], rbuf_e.at[src], e_s.at[k], e_r.at[src], "seq", d)

    loop(1, nseq, lambda k: e_copy(k, lax.rem(me + k, nseq), me).start())
    acc[...] = sbuf_e[me].astype(F32)

    def gather_e(k):
        p = lax.rem(me + nseq - k, nseq)
        e_copy(k, p, p).wait_recv()
        acc[...] += rbuf_e[p].astype(F32)

    loop(1, nseq, gather_e)
    part_f[...] = acc[...].astype(BF16).reshape(part_f.shape)

    def f_copy(k, d, src):
        return to(part_f.at[d], recv_f.at[src], f_s.at[k], f_r.at[src], "grp", d)

    loop(1, ngrp, lambda k: f_copy(k, lax.rem(grp + k, ngrp), grp).start())
    recv_f[grp] = part_f[grp]

    def f_done(k):
        p = lax.rem(grp + ngrp - k, ngrp)
        f_copy(k, p, p).wait_recv()

    loop(1, ngrp, f_done)

    def g_copy(k, d, h, at, src):
        return to(recv_f, slots_hbm.at[:, h, :, at], g_s.at[k], g_r.at[src], "seq", d)

    loop(1, nseq, lambda k: g_copy(k, lax.rem(me + k, nseq), half, pl.ds(col, cw), me).start())
    own = pltpu.make_async_copy(recv_f, slots_hbm.at[:, half, :, pl.ds(col, cw)], own_sem)
    own.start()

    def g_done(k):
        p = lax.rem(me + nseq - k, nseq)
        at = pl.ds(pl.multiple_of(lax.rem(p, cblocks) * cw, cw), cw)
        g_copy(k, p, p // cblocks, at, p).wait_recv()

    loop(1, nseq, g_done)
    own.wait()
    mix_copy.wait()

    def sent(k):
        d = lax.rem(me + k, nseq)
        stat_copy(k, d, me).wait_send()
        a_copy(k, d, me).wait_send()
        c_copy(k, d, half, pl.ds(col, cw), me).wait_send()
        e_copy(k, d, me).wait_send()
        g_copy(k, d, half, pl.ds(col, cw), me).wait_send()

    loop(1, nseq, sent)

    def sent_grp(k):
        d = lax.rem(grp + k, ngrp)
        b_copy(k, d, grp).wait_send()
        f_copy(k, d, grp).wait_send()

    loop(1, ngrp, sent_grp)


def mix_kernel(mix_ref, slots_ref, out_ref):
    for n in range(out_ref.shape[1] // 768):
        at = slice(n * 768, (n + 1) * 768)
        out_ref[:, at] = jnp.dot(
            mix_ref[...], slots_ref[:, at], preferred_element_type=F32
        ).astype(BF16)


def body(tokens, block_map, slot_keys, gate_weight, up_weight, down_weight):
    _, rows, width = tokens.shape
    slots = slot_keys.shape[1]
    nseq = lax.axis_size("seq")
    ngrp = lax.axis_size("grp")
    cw = width // (nseq // 2)
    per_expert = slots // (2 * ngrp)
    part = (ngrp, per_expert, cw)
    flat = (nseq, ngrp * per_expert, cw)
    anywhere = pl.BlockSpec(memory_space=pl.ANY)
    mix, seq_slots = pl.pallas_call(
        functools.partial(layer_kernel, (nseq, ngrp, 3 * slots // 4)),
        out_shape=(
            jax.ShapeDtypeStruct((rows, slots), BF16),
            jax.ShapeDtypeStruct((ngrp, 2, per_expert, width), BF16),
        ),
        in_specs=[anywhere, pl.BlockSpec(memory_space=pltpu.SMEM)] + [anywhere] * 4,
        out_specs=(anywhere, anywhere),
        scratch_shapes=[
            pltpu.VMEM((rows, width), BF16),
            pltpu.VMEM(slot_keys.shape, BF16),
            pltpu.VMEM(gate_weight.shape, BF16),
            pltpu.VMEM(up_weight.shape, BF16),
            pltpu.VMEM(down_weight.shape, BF16),
            pltpu.VMEM((rows, slots), F32),
            pltpu.VMEM((slots, rows), BF16),
            pltpu.VMEM((rows, slots), BF16),
            pltpu.VMEM((slots, width), F32),
            pltpu.VMEM((slots, BLOCK), F32),
            pltpu.VMEM((nseq, 2, slots), F32),
            pltpu.VMEM(flat, BF16),
            pltpu.VMEM(flat, BF16),
            pltpu.VMEM(part, BF16),
            pltpu.VMEM(part, BF16),
            pltpu.VMEM((2, ngrp, per_expert, width), BF16),
            pltpu.VMEM(flat, BF16),
            pltpu.VMEM(flat, BF16),
            pltpu.VMEM(part, BF16),
            pltpu.VMEM(part, BF16),
            pltpu.VMEM(flat[1:], F32),
            pltpu.SemaphoreType.DMA((4,)),
            pltpu.SemaphoreType.DMA((4,)),
            pltpu.SemaphoreType.DMA,
            pltpu.SemaphoreType.DMA,
        ]
        + [
            pltpu.SemaphoreType.DMA((n,))
            for n in (nseq, nseq, nseq, nseq, ngrp, ngrp, nseq, nseq)
            + (nseq, nseq, ngrp, ngrp, nseq, nseq)
        ],
        compiler_params=pltpu.CompilerParams(
            collective_id=0, has_side_effects=True, vmem_limit_bytes=52 << 20
        ),
    )(tokens, block_map, slot_keys, gate_weight, up_weight, down_weight)

    tile = rows // 4
    out = pl.pallas_call(
        mix_kernel,
        grid=(4,),
        out_shape=jax.ShapeDtypeStruct((rows, width), BF16),
        in_specs=[
            pl.BlockSpec((tile, slots), lambda i: (i, 0)),
            pl.BlockSpec((slots, width), lambda i: (0, 0)),
        ],
        out_specs=pl.BlockSpec((tile, width), lambda i: (i, 0)),
        compiler_params=pltpu.CompilerParams(vmem_limit_bytes=24 << 20),
    )(mix, seq_slots.reshape(slots, width))
    return out[None]


def solution(mesh):
    placed = (
        P("grp", "seq", None),
        P("grp", "seq"),
        P(),
        P("grp", None, "seq"),
        P("grp", None, "seq"),
        P("grp", "seq", None),
    )
    return jax.shard_map(
        body, mesh=mesh, in_specs=placed, out_specs=P("grp", "seq", None), check_vma=False
    )
```

time: 276 us -> 123 us (0.45)
  the two profiles are of different devices: /device:TPU:0 before, /device:TPU:24 now
where the time goes in v1:
time: 123 us
  Pallas kernels  121 us (98%)
  local copies, waits for them, and re-layouts  2.06 us (2%)
    pallas_call x1, Pallas kernels, body(): pl.pallas_call(functools.partial(layer_kernel, (nseq, ngrp, 3 * slots //...  117 us
    pallas_call x1, Pallas kernels, body(): pl.pallas_call(mix_kernel, grid=(4,), out_shape=jax.ShapeDtypeStruct((row...  4.03 us

profile of v1, /device:TPU:24, one launch (start us, length us, event | category | flops | bytes accessed | tf_op | source)
XLA Modules:
  0.0 123.0 jit_solution(7393382832477384153)
XLA Ops:
  0.0 0.0 copy-start.1
  0.0 0.7 copy-done.1
  0.7 116.8 %shard_map.64 = (bf16[1024,256]{1,0:T(8,128)(2,1)S(1)}, bf16[8,2,16,3072]{3,2,1,0:T(8,128)(2,1)}) custom-call(bf16[1,1024,3072]{2,1,0:T(8,128)(2,1)} %tok_hbm.1, s32[1,8]{1,0:T(1,128)S(1)} %copy-done.1, bf16[3072,256]{1,0:T(8,128)(2,1)} %keys_hbm.1, bf16[2,3072,256]{2,1,0:T(8,128)(2,1)} %wg_hbm.1, bf16[2,3072,256]{2,1,0:T(8,128)(2,1)} %wu_hbm.1, ...), custom_call_target="tpu_custom_call" | custom-call | tf_op jit(solution)/shard_map/pallas_call | solution.py:349
  117.5 0.0 copy-start
  117.5 1.4 %copy-done = bf16[8,2,16,3072]{3,2,1,0:T(8,128)(2,1)S(1)} copy-done((bf16[8,2,16,3072]{3,2,1,0:T(8,128)(2,1)S(1)}, bf16[8,2,16,3072]{3,2,1,0:T(8,128)(2,1)}, u32[]{:S(2)}) %copy-start) | copy-done | bytes 1572888
  118.9 4.0 %shard_map.65 = bf16[1024,3072]{1,0:T(8,128)(2,1)} custom-call(bf16[1024,256]{1,0:T(8,128)(2,1)S(1)} %get-tuple-element.7.mix_ref, bf16[256,3072]{1,0:T(8,128)(2,1)S(1)} %bitcast.2), custom_call_target="tpu_custom_call" | custom-call | tf_op jit(solution)/shard_map/pallas_call | solution.py:395
Async XLA Ops:
  0.0 0.7 copy-start.1
  117.5 1.4 %copy-start = (bf16[8,2,16,3072]{3,2,1,0:T(8,128)(2,1)S(1)}, bf16[8,2,16,3072]{3,2,1,0:T(8,128)(2,1)}, u32[]{:S(2)}) copy-start(bf16[8,2,16,3072]{3,2,1,0:T(8,128)(2,1)} %get-tuple-element.8) | copy-start | bytes 4718596

commit v2 on v1

v2 whole, which is shorter than its diff:
```python
import functools
import jax
import jax.numpy as jnp
from jax import lax
from jax.experimental import pallas as pl
from jax.experimental.pallas import tpu as pltpu
from jax.sharding import PartitionSpec as P

BLOCK = 128
SIDE = 4
CHUNKS = 3
MESH = pl.DeviceIdType.MESH
F32 = jnp.float32
BF16 = jnp.bfloat16


def loop(start, stop, fn):
    def step(k, carry):
        fn(k)
        return carry

    lax.fori_loop(start, stop, step, 0)


def layer_kernel(
    dims,
    tok_hbm,
    bm_hbm,
    keys_hbm,
    wg_hbm,
    wu_hbm,
    wd_hbm,
    mix_hbm,
    slots_hbm,
    tok,
    bm,
    keys,
    wg,
    wu,
    wd,
    logits,
    wts,
    mixb,
    fac,
    stat,
    terms,
    first,
    middle,
    second,
    grp_out,
    grp_in,
    xs,
    gates,
    ups,
    ys,
    tok_sem,
    in_sem,
    mix_sem,
    own_sem,
    stat_s,
    stat_r,
    sum_hs,
    sum_hr,
    sum_ls,
    sum_lr,
    grp_s,
    grp_r,
    put_ls,
    put_lr,
    put_hs,
    put_hr,
):
    nseq, ngrp, image_slots = dims
    me = lax.axis_index("seq")
    grp = lax.axis_index("grp")
    rows, width = tok.shape
    slots = keys.shape[1]
    tchunk = rows // 4
    blocks = rows // BLOCK
    cw = width // CHUNKS
    bw = cw // 2
    pw = bw // SIDE
    prow = slots // 4
    at_x, at_y = me // SIDE, lax.rem(me, SIDE)
    place = ((at_x, at_y), (at_y, at_x))

    def seq_of(h, u, v):
        return u * SIDE + v if h == 0 else v * SIDE + u

    def block_cols(s, u):
        return pl.ds(pl.multiple_of(s * cw + lax.rem(u, 2) * bw, bw), bw)

    def piece_cols(s, u, v):
        return pl.ds(pl.multiple_of(s * cw + lax.rem(u, 2) * bw + v * pw, pw), pw)

    def piece_at(v):
        return pl.ds(pl.multiple_of(v * pw, pw), pw)

    bm_copy = pltpu.make_async_copy(bm_hbm, bm, in_sem.at[4])
    bm_copy.start()
    keys_copy = pltpu.make_async_copy(keys_hbm, keys, in_sem.at[0])
    keys_copy.start()

    def tok_copy(r):
        at = pl.ds(pl.multiple_of(r * tchunk, tchunk), tchunk)
        return pltpu.make_async_copy(tok_hbm.at[0, at], tok.at[at], tok_sem.at[r])

    loop(0, 4, lambda r: tok_copy(r).start())
    wg_copy = pltpu.make_async_copy(wg_hbm, wg, in_sem.at[1])
    wu_copy = pltpu.make_async_copy(wu_hbm, wu, in_sem.at[2])
    wd_copy = pltpu.make_async_copy(wd_hbm, wd, in_sem.at[3])

    barrier = pltpu.get_barrier_semaphore()

    def greet(axis, n, mine):
        def go(k):
            pl.semaphore_signal(
                barrier, inc=1, device_id={axis: lax.rem(mine + k, n)}, device_id_type=MESH
            )

        loop(1, n, go)

    greet("seq", nseq, me)
    greet("grp", ngrp, grp)

    def to(src, dst, ssem, rsem, axis, peer):
        return pltpu.make_async_remote_copy(
            src_ref=src,
            dst_ref=dst,
            send_sem=ssem,
            recv_sem=rsem,
            device_id={axis: peer},
            device_id_type=MESH,
        )

    text_lane = (lax.broadcasted_iota(jnp.int32, (1, slots), 1) >= image_slots).astype(jnp.int32)

    def by_stream(x):
        wide = slots // 16
        return jnp.concatenate(
            [
                x[(2 * g + h) * 16 + t * 8 : (2 * g + h) * 16 + t * 8 + 8]
                for h in range(2)
                for t in range(2)
                for g in range(wide // 2)
            ],
            axis=0,
        )

    bm_copy.wait()
    keys_copy.wait()
    per = tchunk // BLOCK

    def logit_chunk(r, peak):
        tok_copy(r).wait()
        at = pl.ds(pl.multiple_of(r * tchunk, tchunk), tchunk)
        got = jnp.dot(tok[at], keys[...], preferred_element_type=F32)
        for b in range(per):
            block = jnp.where(
                text_lane == bm[0, r * per + b], got[b * BLOCK : (b + 1) * BLOCK], -1e30
            )
            logits[pl.ds(pl.multiple_of(r * tchunk + b * BLOCK, BLOCK), BLOCK)] = block
            peak = jnp.maximum(peak, jnp.max(block, axis=0, keepdims=True))
        return peak

    peak = lax.fori_loop(0, 4, logit_chunk, jnp.full((1, slots), -1e30, F32))
    wg_copy.start()
    wu_copy.start()
    wd_copy.start()

    def weigh(b, total):
        at = pl.ds(pl.multiple_of(b * BLOCK, BLOCK), BLOCK)
        w = jnp.where(text_lane == bm[0, b], jnp.exp(logits[at] - peak), 0.0)
        wts[:, at] = by_stream(w.T).astype(BF16)
        return total + jnp.sum(w, axis=0, keepdims=True)

    total = lax.fori_loop(0, blocks, weigh, jnp.zeros((1, slots), F32))
    stat[me, 0:1] = peak
    stat[me, 1:2] = total

    pl.semaphore_wait(barrier, nseq - 1 + ngrp - 1)

    def stat_copy(k, peer, src):
        return to(stat.at[src], stat.at[src], stat_s.at[k], stat_r.at[src], "seq", peer)

    loop(1, nseq, lambda k: stat_copy(k, lax.rem(me + k, nseq), me).start())

    def around(n, at, k):
        return lax.rem(at + k, n)

    def before(n, at, k):
        return lax.rem(at + n - k, n)

    def sum_heavy(p, h, s, k, dst, src):
        _, v = place[h]
        return to(
            terms.at[p, h, dst // 2, :, block_cols(s, dst)],
            first.at[p, h, s, src],
            sum_hs.at[p, h, s, k],
            sum_hr.at[p, h, s, src],
            "seq",
            seq_of(h, dst, v),
        )

    def sum_light(p, h, s, k, dst, src):
        u, _ = place[h]
        return to(
            middle.at[p, h, s, :, piece_at(dst)],
            second.at[p, h, s, src],
            sum_ls.at[p, h, s, k],
            sum_lr.at[p, h, s, src],
            "seq",
            seq_of(h, u, dst),
        )

    def swap(p, h, s, k, dst, src):
        return to(
            grp_out.at[p, h, s, dst],
            grp_in.at[p, h, s, src],
            grp_s.at[p, h, s, k],
            grp_r.at[p, h, s, src],
            "grp",
            dst,
        )

    def put_light(p, h, s, k, dst, src):
        u, v = place[h]
        if p == 0:
            here = xs.at[h, u // 2, :, piece_cols(s, u, v)]
            there = xs.at[h, u // 2, :, piece_cols(s, u, src)]
        else:
            here = ys.at[h, s, :, :, piece_at(v)]
            there = ys.at[h, s, :, :, piece_at(src)]
        return to(
            here,
            there,
            put_ls.at[p, h, s, k],
            put_lr.at[p, h, s, src],
            "seq",
            seq_of(h, u, dst),
        )

    def put_heavy(p, h, s, k, dst, src):
        u, v = place[h]
        if p == 0:
            here = xs.at[h, u // 2, :, block_cols(s, u)]
            there = xs.at[h, src // 2, :, block_cols(s, src)]
        else:
            here = ys.at[h, s]
            there = slots_hbm.at[:, h, src // 2, :, block_cols(s, src)]
        return to(
            here,
            there,
            put_hs.at[p, h, s, k],
            put_hr.at[p, h, s, src],
            "seq",
            seq_of(h, dst, v),
        )

    def own_copy(h, s):
        u, _ = place[h]
        return pltpu.make_async_copy(
            ys.at[h, s], slots_hbm.at[:, h, u // 2, :, block_cols(s, u)], own_sem.at[h, s]
        )

    def start_sum(p, h, s):
        u, _ = place[h]
        loop(1, SIDE, lambda k: sum_heavy(p, h, s, k, around(SIDE, u, k), u).start())

    def mid_sum(p, h, s):
        u, v = place[h]
        acc = terms[p, h, u // 2, :, block_cols(s, u)].astype(F32)
        scale = [None] * SIDE
        if p == 0:
            mine = fac[pl.ds(pl.multiple_of(h * 2 * prow + (u // 2) * prow, prow), prow)]
            scale = [mine[:, h * SIDE + k : h * SIDE + k + 1] for k in range(SIDE)]
            acc = acc * scale[0]
        for k in range(1, SIDE):
            src = before(SIDE, u, k)
            sum_heavy(p, h, s, k, src, src).wait_recv()
            got = first[p, h, s, src].astype(F32)
            acc = acc + (got if p else got * scale[k])
        middle[p, h, s] = acc.astype(BF16)
        loop(1, SIDE, lambda k: sum_light(p, h, s, k, around(SIDE, v, k), v).start())

    def end_sum(p, h, s):
        _, v = place[h]
        acc = middle[p, h, s, :, piece_at(v)].astype(F32)
        for k in range(1, SIDE):
            src = before(SIDE, v, k)
            sum_light(p, h, s, k, src, src).wait_recv()
            acc = acc + second[p, h, s, src].astype(F32)
        grp_out[p, h, s] = acc.reshape(grp_out.shape[3:]).astype(BF16)
        loop(1, ngrp, lambda k: swap(p, h, s, k, around(ngrp, grp, k), grp).start())
        grp_in[p, h, s, grp] = grp_out[p, h, s, grp]

    def start_put(p, h, s):
        u, v = place[h]
        for k in range(1, ngrp):
            src = before(ngrp, grp, k)
            swap(p, h, s, k, src, src).wait_recv()
        if p == 0:
            xs[h, u // 2, :, piece_cols(s, u, v)] = grp_in[p, h, s].reshape(prow, pw)
        else:
            ys[h, s, :, :, piece_at(v)] = grp_in[p, h, s]
        loop(1, SIDE, lambda k: put_light(p, h, s, k, around(SIDE, v, k), v).start())

    def mid_put(p, h, s):
        u, v = place[h]
        for k in range(1, SIDE):
            src = before(SIDE, v, k)
            put_light(p, h, s, k, src, src).wait_recv()
        loop(1, SIDE, lambda k: put_heavy(p, h, s, k, around(SIDE, u, k), u).start())
        if p == 1:
            own_copy(h, s).start()

    def end_put(p, h, s):
        u, _ = place[h]
        for k in range(1, SIDE):
            src = before(SIDE, u, k)
            put_heavy(p, h, s, k, src, src).wait_recv()
        if p == 1:
            own_copy(h, s).wait()
            return
        x = xs[h, :, :, s * cw : (s + 1) * cw].reshape(2 * prow, cw)
        gate = jnp.dot(x, wg[h, s * cw : (s + 1) * cw], preferred_element_type=F32)
        up = jnp.dot(x, wu[h, s * cw : (s + 1) * cw], preferred_element_type=F32)
        if s > 0:
            gate = gate + gates[h]
            up = up + ups[h]
        if s < CHUNKS - 1:
            gates[h] = gate
            ups[h] = up
            return
        hidden = (gate / (1.0 + jnp.exp(-gate)) * up).astype(BF16)
        for n in range(CHUNKS):
            at = slice(n * cw, (n + 1) * cw)
            out = jnp.dot(hidden, wd[h, :, at], preferred_element_type=F32)
            terms[1, h, :, :, at] = out.reshape(2, prow, cw).astype(BF16)
            start_sum(1, h, n)

    def mix_rows(b):
        at = pl.ds(pl.multiple_of(b * BLOCK, BLOCK), BLOCK)
        m = logits[at]
        e = jnp.where(text_lane == bm[0, b], jnp.exp(m - jnp.max(m, axis=1, keepdims=True)), 0.0)
        mixb[at] = (e / jnp.sum(e, axis=1, keepdims=True)).astype(BF16)

    for s in range(CHUNKS):
        at = slice(s * cw, (s + 1) * cw)
        out = jnp.dot(wts[...], tok[:, at], preferred_element_type=F32)
        terms[0, :, :, :, at] = out.reshape(2, 2, prow, cw).astype(BF16)
        for h in range(2):
            start_sum(0, h, s)

    def stat_done(k):
        src = before(nseq, me, k)
        stat_copy(k, src, src).wait_recv()

    loop(1, nseq, stat_done)
    peaks = stat[:, 0, :]
    top = jnp.max(peaks, axis=0, keepdims=True)
    whole = jnp.sum(jnp.exp(peaks - top) * stat[:, 1, :], axis=0, keepdims=True)
    near = []
    for h in range(2):
        u, v = place[h]
        for k in range(SIDE):
            near.append(stat[seq_of(h, before(SIDE, u, k), v), 0:1])
    near = jnp.exp(jnp.concatenate(near, axis=0) - top) / whole
    fac[...] = by_stream(jnp.concatenate([near] * (BLOCK // (2 * SIDE)), axis=0).T)

    steps = (mid_sum, end_sum, start_put, mid_put, end_put)
    mix_copy = pltpu.make_async_copy(mixb, mix_hbm, mix_sem)

    for p in range(2):
        for tick in range(len(steps) + CHUNKS - 1):
            for n in reversed(range(len(steps))):
                s = tick - n
                if 0 <= s < CHUNKS:
                    for h in range(2):
                        steps[n](p, h, s)
            if p == 0 and tick == CHUNKS:
                wg_copy.wait()
                wu_copy.wait()
                wd_copy.wait()
                loop(0, blocks, mix_rows)
                mix_copy.start()

    mix_copy.wait()

    def stat_sent(k):
        stat_copy(k, around(nseq, me, k), me).wait_send()

    loop(1, nseq, stat_sent)
    for p in range(2):
        for h in range(2):
            u, v = place[h]

            def sent(s):
                for k in range(1, SIDE):
                    sum_heavy(p, h, s, k, around(SIDE, u, k), u).wait_send()
                    sum_light(p, h, s, k, around(SIDE, v, k), v).wait_send()
                    put_light(p, h, s, k, around(SIDE, v, k), v).wait_send()
                    put_heavy(p, h, s, k, around(SIDE, u, k), u).wait_send()
                for k in range(1, ngrp):
                    swap(p, h, s, k, around(ngrp, grp, k), grp).wait_send()

            loop(0, CHUNKS, sent)


def mix_kernel(mix_ref, slots_ref, out_ref):
    step = out_ref.shape[1] // CHUNKS
    for n in range(CHUNKS):
        at = slice(n * step, (n + 1) * step)
        out_ref[:, at] = jnp.dot(
            mix_ref[...], slots_ref[:, at], preferred_element_type=F32
        ).astype(BF16)


def body(tokens, block_map, slot_keys, gate_weight, up_weight, down_weight):
    _, rows, width = tokens.shape
    slots = slot_keys.shape[1]
    nseq = lax.axis_size("seq")
    ngrp = lax.axis_size("grp")
    hidden = gate_weight.shape[2]
    cw = width // CHUNKS
    bw = cw // 2
    pw = bw // SIDE
    prow = slots // 4
    per = prow // ngrp
    anywhere = pl.BlockSpec(memory_space=pl.ANY)
    streams = (2, 2, CHUNKS)
    dma = pltpu.SemaphoreType.DMA
    mix, seq_slots = pl.pallas_call(
        functools.partial(layer_kernel, (nseq, ngrp, 3 * slots // 4)),
        out_shape=(
            jax.ShapeDtypeStruct((rows, slots), BF16),
            jax.ShapeDtypeStruct((ngrp, 2, 2, per, width), BF16),
        ),
        in_specs=[anywhere] * 6,
        out_specs=(anywhere, anywhere),
        scratch_shapes=[
            pltpu.VMEM((rows, width), BF16),
            pltpu.SMEM(block_map.shape, jnp.int32),
            pltpu.VMEM(slot_keys.shape, BF16),
            pltpu.VMEM(gate_weight.shape, BF16),
            pltpu.VMEM(up_weight.shape, BF16),
            pltpu.VMEM(down_weight.shape, BF16),
            pltpu.VMEM((rows, slots), F32),
            pltpu.VMEM((slots, rows), BF16),
            pltpu.VMEM((rows, slots), BF16),
            pltpu.VMEM((slots, BLOCK), F32),
            pltpu.VMEM((nseq, 2, slots), F32),
            pltpu.VMEM((2, 2, 2, prow, width), BF16),
            pltpu.VMEM((*streams, SIDE, prow, bw), BF16),
            pltpu.VMEM((*streams, prow, bw), BF16),
            pltpu.VMEM((*streams, SIDE, prow, pw), BF16),
            pltpu.VMEM((*streams, ngrp, per, pw), BF16),
            pltpu.VMEM((*streams, ngrp, per, pw), BF16),
            pltpu.VMEM((2, 2, prow, width), BF16),
            pltpu.VMEM((2, 2 * prow, hidden), F32),
            pltpu.VMEM((2, 2 * prow, hidden), F32),
            pltpu.VMEM((2, CHUNKS, ngrp, per, bw), BF16),
            dma((4,)),
            dma((5,)),
            dma,
            dma((2, CHUNKS)),
            dma((nseq,)),
            dma((nseq,)),
            dma((*streams, SIDE)),
            dma((*streams, SIDE)),
            dma((*streams, SIDE)),
            dma((*streams, SIDE)),
            dma((*streams, ngrp)),
            dma((*streams, ngrp)),
            dma((*streams, SIDE)),
            dma((*streams, SIDE)),
            dma((*streams, SIDE)),
            dma((*streams, SIDE)),
        ],
        compiler_params=pltpu.CompilerParams(
            collective_id=0, has_side_effects=True, vmem_limit_bytes=52 << 20
        ),
    )(tokens, block_map, slot_keys, gate_weight, up_weight, down_weight)

    tile = rows // 4
    out = pl.pallas_call(
        mix_kernel,
        grid=(4,),
        out_shape=jax.ShapeDtypeStruct((rows, width), BF16),
        in_specs=[
            pl.BlockSpec((tile, slots), lambda i: (i, 0)),
            pl.BlockSpec((slots, width), lambda i: (0, 0)),
        ],
        out_specs=pl.BlockSpec((tile, width), lambda i: (i, 0)),
        compiler_params=pltpu.CompilerParams(vmem_limit_bytes=60 << 20),
    )(mix, seq_slots.reshape(slots, width))
    return out[None]


def solution(mesh):
    placed = (
        P("grp", "seq", None),
        P("grp", "seq"),
        P(),
        P("grp", None, "seq"),
        P("grp", None, "seq"),
        P("grp", "seq", None),
    )
    return jax.shard_map(
        body, mesh=mesh, in_specs=placed, out_specs=P("grp", "seq", None), check_vma=False
    )
```

time: 123 us -> 92.5 us (0.75)
  the two profiles are of different devices: /device:TPU:24 before, /device:TPU:0 now
where the time goes in v2:
time: 92.5 us; the launch traced here: 92.3 us
  Pallas kernels  90.9 us (98%)
  local copies, waits for them, and re-layouts  1.45 us (2%)
    pallas_call x1, Pallas kernels, body(): pl.pallas_call(functools.partial(layer_kernel, (nseq, ngrp, 3 * slots //...  85 us
    pallas_call x1, Pallas kernels, body(): pl.pallas_call(mix_kernel, grid=(4,), out_shape=jax.ShapeDtypeStruct((row...  5.83 us

profile of v2, /device:TPU:0, one launch (start us, length us, event | category | flops | bytes accessed | tf_op | source)
XLA Modules:
  0.0 92.3 jit_solution(9967927687302459450)
XLA Ops:
  0.0 0.0 copy-start.1
  0.0 0.7 copy-done.1
  0.7 85.0 %shard_map.64 = (bf16[1024,256]{1,0:T(8,128)(2,1)S(1)}, bf16[8,2,2,8,3072]{4,3,2,1,0:T(8,128)(2,1)}) custom-call(bf16[1,1024,3072]{2,1,0:T(8,128)(2,1)} %tok_hbm.1, s32[1,8]{1,0:T(1,128)S(1)} %copy-done.1, bf16[3072,256]{1,0:T(8,128)(2,1)} %keys_hbm.1, bf16[2,3072,256]{2,1,0:T(8,128)(2,1)} %wg_hbm.1, bf16[2,3072,256]{2,1,0:T(8,128)(2,1)} %wu_hbm.1, ...), custom_call_target="tpu_custom_call" | custom-call | tf_op jit(solution)/shard_map/pallas_call | solution.py:433
  85.7 0.0 copy-start
  85.7 0.8 copy-done
  86.5 5.8 %shard_map.65 = bf16[1024,3072]{1,0:T(8,128)(2,1)} custom-call(bf16[1024,256]{1,0:T(8,128)(2,1)} %copy-done, bf16[256,3072]{1,0:T(8,128)(2,1)} %bitcast.2), custom_call_target="tpu_custom_call" | custom-call | tf_op jit(solution)/shard_map/pallas_call | solution.py:486
Async XLA Ops:
  0.0 0.7 copy-start.1
  85.7 0.8 copy-start

commit v3 on v2

v3 whole, which is shorter than its diff:
```python
import functools
import jax
import jax.numpy as jnp
from jax import lax
from jax.experimental import pallas as pl
from jax.experimental.pallas import tpu as pltpu
from jax.sharding import PartitionSpec as P

BLOCK = 128
SIDE = 4
CHUNKS = 3
MESH = pl.DeviceIdType.MESH
F32 = jnp.float32
BF16 = jnp.bfloat16


def loop(start, stop, fn):
    def step(k, carry):
        fn(k)
        return carry

    lax.fori_loop(start, stop, step, 0)


def layer_kernel(
    dims,
    tok_hbm,
    bm_hbm,
    keys_hbm,
    wg_hbm,
    wu_hbm,
    wd_hbm,
    mix_hbm,
    slots_hbm,
    tok,
    bm,
    keys,
    wg,
    wu,
    wd,
    logits,
    wts,
    mixb,
    fac,
    scales,
    stat,
    terms,
    first,
    middle,
    second,
    xs,
    gates,
    ups,
    ys,
    tok_sem,
    in_sem,
    mix_sem,
    own_sem,
    sent,
    stat_r,
    sum_hr,
    sum_lr,
    put_lr,
    put_hr,
):
    nseq, ngrp, image_slots = dims
    me = lax.axis_index("seq")
    grp = lax.axis_index("grp")
    rows, width = tok.shape
    slots = keys.shape[1]
    tchunk = rows // 4
    blocks = rows // BLOCK
    cw = width // CHUNKS
    bw = cw // 2
    pw = bw // SIDE
    prow = slots // 4
    at_x, at_y = me // SIDE, lax.rem(me, SIDE)
    place = ((at_x, at_y), (at_y, at_x))

    def seq_of(h, u, v):
        return u * SIDE + v if h == 0 else v * SIDE + u

    def block_cols(s, u):
        return pl.ds(pl.multiple_of(s * cw + lax.rem(u, 2) * bw, bw), bw)

    def piece_cols(s, u, v):
        return pl.ds(pl.multiple_of(s * cw + lax.rem(u, 2) * bw + v * pw, pw), pw)

    def piece_at(v):
        return pl.ds(pl.multiple_of(v * pw, pw), pw)

    bm_copy = pltpu.make_async_copy(bm_hbm, bm, in_sem.at[4])
    bm_copy.start()
    keys_copy = pltpu.make_async_copy(keys_hbm, keys, in_sem.at[0])
    keys_copy.start()

    def tok_copy(r):
        at = pl.ds(pl.multiple_of(r * tchunk, tchunk), tchunk)
        return pltpu.make_async_copy(tok_hbm.at[0, at], tok.at[at], tok_sem.at[r])

    loop(0, 4, lambda r: tok_copy(r).start())
    wg_copy = pltpu.make_async_copy(wg_hbm, wg, in_sem.at[1])
    wu_copy = pltpu.make_async_copy(wu_hbm, wu, in_sem.at[2])
    wd_copy = pltpu.make_async_copy(wd_hbm, wd, in_sem.at[3])

    barrier = pltpu.get_barrier_semaphore()

    def greet(peer):
        pl.semaphore_signal(barrier, inc=1, device_id=peer, device_id_type=MESH)

    for h in range(2):
        u, v = place[h]

        def greet_line(k):
            peer = seq_of(h, u, lax.rem(v + k // ngrp, SIDE))
            greet({"seq": peer, "grp": lax.rem(grp + k, ngrp)})

        loop(ngrp if h else 1, SIDE * ngrp, greet_line)

    def greet_rest(k):
        x = lax.rem(at_x + 1 + k // (SIDE - 1), SIDE)
        y = lax.rem(at_y + 1 + lax.rem(k, SIDE - 1), SIDE)
        greet({"seq": x * SIDE + y})

    loop(0, (SIDE - 1) * (SIDE - 1), greet_rest)
    greeted = (2 * SIDE - 1) * ngrp - 1 + (SIDE - 1) * (SIDE - 1)

    def to(src, dst, ssem, rsem, peer, **more):
        return pltpu.make_async_remote_copy(
            src_ref=src,
            dst_ref=dst,
            send_sem=ssem,
            recv_sem=rsem,
            device_id={"seq": peer, **more},
            device_id_type=MESH,
        )

    text_lane = (lax.broadcasted_iota(jnp.int32, (1, slots), 1) >= image_slots).astype(jnp.int32)

    def by_stream(x):
        wide = slots // 16
        return jnp.concatenate(
            [
                x[(2 * g + h) * 16 + t * 8 : (2 * g + h) * 16 + t * 8 + 8]
                for h in range(2)
                for t in range(2)
                for g in range(wide // 2)
            ],
            axis=0,
        )

    bm_copy.wait()
    keys_copy.wait()
    per = tchunk // BLOCK

    def logit_chunk(r, peak):
        tok_copy(r).wait()
        at = pl.ds(pl.multiple_of(r * tchunk, tchunk), tchunk)
        got = jnp.dot(tok[at], keys[...], preferred_element_type=F32)
        for b in range(per):
            block = jnp.where(
                text_lane == bm[0, r * per + b], got[b * BLOCK : (b + 1) * BLOCK], -1e30
            )
            logits[pl.ds(pl.multiple_of(r * tchunk + b * BLOCK, BLOCK), BLOCK)] = block
            peak = jnp.maximum(peak, jnp.max(block, axis=0, keepdims=True))
        return peak

    peak = lax.fori_loop(0, 4, logit_chunk, jnp.full((1, slots), -1e30, F32))
    wg_copy.start()
    wu_copy.start()
    wd_copy.start()

    def weigh(b, total):
        at = pl.ds(pl.multiple_of(b * BLOCK, BLOCK), BLOCK)
        w = jnp.where(text_lane == bm[0, b], jnp.exp(logits[at] - peak), 0.0)
        wts[:, at] = by_stream(w.T).astype(BF16)
        return total + jnp.sum(w, axis=0, keepdims=True)

    total = lax.fori_loop(0, blocks, weigh, jnp.zeros((1, slots), F32))
    stat[me, 0:1] = peak
    stat[me, 1:2] = total

    pl.semaphore_wait(barrier, greeted)

    def stat_copy(peer, src):
        return to(stat.at[src], stat.at[src], sent.at[0, 0], stat_r, peer)

    loop(1, nseq, lambda k: stat_copy(lax.rem(me + k, nseq), me).start())

    def around(n, at, k):
        return lax.rem(at + k, n)

    def before(n, at, k):
        return lax.rem(at + n - k, n)

    def sum_heavy(p, h, s, dst, src):
        _, v = place[h]
        return to(
            terms.at[p, h, dst // 2, :, block_cols(s, dst)],
            first.at[p, h, s, src],
            sent.at[1, p],
            sum_hr.at[p, h, s],
            seq_of(h, dst, v),
        )

    def sum_light(p, h, s, dst, dst_grp, src, src_grp):
        u, _ = place[h]
        return to(
            middle.at[p, h, s, dst_grp, :, piece_at(dst)],
            second.at[p, h, s, src * ngrp + src_grp],
            sent.at[2, p],
            sum_lr.at[p, h, s],
            seq_of(h, u, dst),
            grp=dst_grp,
        )

    def put_light(p, h, s, dst, src):
        u, v = place[h]
        if p == 0:
            here = xs.at[h, u // 2, :, piece_cols(s, u, v)]
            there = xs.at[h, u // 2, :, piece_cols(s, u, src)]
        else:
            here = ys.at[h, s, :, :, piece_at(v)]
            there = ys.at[h, s, :, :, piece_at(src)]
        return to(
            here,
            there,
            sent.at[3, p],
            put_lr.at[p, h, s],
            seq_of(h, u, dst),
        )

    def put_heavy(p, h, s, dst, src):
        u, v = place[h]
        if p == 0:
            here = xs.at[h, u // 2, :, block_cols(s, u)]
            there = xs.at[h, src // 2, :, block_cols(s, src)]
        else:
            here = ys.at[h, s]
            there = slots_hbm.at[:, h, src // 2, :, block_cols(s, src)]
        return to(
            here,
            there,
            sent.at[4, p],
            put_hr.at[p, h, s],
            seq_of(h, dst, v),
        )

    def own_copy(h, s):
        u, _ = place[h]
        return pltpu.make_async_copy(
            ys.at[h, s], slots_hbm.at[:, h, u // 2, :, block_cols(s, u)], own_sem.at[h, s]
        )

    def start_sum(p, h, s):
        u, _ = place[h]
        loop(1, SIDE, lambda k: sum_heavy(p, h, s, around(SIDE, u, k), u).start())

    def arrived(ref, sem):
        pltpu.make_async_copy(ref, ref, sem).wait()

    def mid_sum(p, h, s):
        u, v = place[h]
        acc = terms[p, h, u // 2, :, block_cols(s, u)].astype(F32)
        arrived(first.at[p, h, s, : SIDE - 1], sum_hr.at[p, h, s])
        if p == 0:
            acc = acc * scale_of(h, 0)
        for k in range(1, SIDE):
            got = first[p, h, s, before(SIDE, u, k)].astype(F32)
            acc = acc + (got if p else got * scale_of(h, k))
        middle[p, h, s] = acc.reshape(middle.shape[3:]).astype(BF16)

        def send(k):
            dst, dst_grp = around(SIDE, v, k // ngrp), around(ngrp, grp, k)
            sum_light(p, h, s, dst, dst_grp, v, grp).start()

        loop(1, SIDE * ngrp, send)
        second[p, h, s, v * ngrp + grp] = middle[p, h, s, grp, :, piece_at(v)]

    def scale_of(h, k):
        return jnp.concatenate([scales[h, k]] * (bw // BLOCK), axis=1)

    def end_sum(p, h, s):
        u, v = place[h]
        arrived(second.at[p, h, s, : SIDE * ngrp - 1], sum_lr.at[p, h, s])
        acc = second[p, h, s, :ngrp].astype(F32)
        for k in range(1, SIDE):
            acc = acc + second[p, h, s, k * ngrp : (k + 1) * ngrp].astype(F32)
        if p == 0:
            piece = acc.reshape(prow, pw).astype(BF16)
            xs[h, u // 2, :, piece_cols(s, u, v)] = piece
        else:
            ys[h, s, :, :, piece_at(v)] = acc.astype(BF16)
        loop(1, SIDE, lambda k: put_light(p, h, s, around(SIDE, v, k), v).start())

    def mid_put(p, h, s):
        u, v = place[h]
        arrived(ys.at[h, s, :, :, : (SIDE - 1) * pw], put_lr.at[p, h, s])
        loop(1, SIDE, lambda k: put_heavy(p, h, s, around(SIDE, u, k), u).start())
        if p == 1:
            own_copy(h, s).start()

    def end_put(p, h, s):
        arrived(first.at[p, h, s, : SIDE - 1], put_hr.at[p, h, s])
        if p == 1:
            own_copy(h, s).wait()
            return
        x = xs[h, :, :, s * cw : (s + 1) * cw].reshape(2 * prow, cw)
        gate = jnp.dot(x, wg[h, s * cw : (s + 1) * cw], preferred_element_type=F32)
        up = jnp.dot(x, wu[h, s * cw : (s + 1) * cw], preferred_element_type=F32)
        if s > 0:
            gate = gate + gates[h]
            up = up + ups[h]
        if s < CHUNKS - 1:
            gates[h] = gate
            ups[h] = up
            return
        hidden = (gate / (1.0 + jnp.exp(-gate)) * up).astype(BF16)
        for n in range(CHUNKS):
            at = slice(n * cw, (n + 1) * cw)
            out = jnp.dot(hidden, wd[h, :, at], preferred_element_type=F32)
            terms[1, h, :, :, at] = out.reshape(2, prow, cw).astype(BF16)
            if n < CHUNKS - 1:
                start_sum(1, h, n)

    def mix_rows(b):
        at = pl.ds(pl.multiple_of(b * BLOCK, BLOCK), BLOCK)
        m = logits[at]
        e = jnp.where(text_lane == bm[0, b], jnp.exp(m - jnp.max(m, axis=1, keepdims=True)), 0.0)
        mixb[at] = (e / jnp.sum(e, axis=1, keepdims=True)).astype(BF16)

    for s in range(CHUNKS):
        at = slice(s * cw, (s + 1) * cw)
        out = jnp.dot(wts[...], tok[:, at], preferred_element_type=F32)
        terms[0, :, :, :, at] = out.reshape(2, 2, prow, cw).astype(BF16)
        if s < CHUNKS - 1:
            for h in range(2):
                start_sum(0, h, s)

    loop(0, blocks, mix_rows)
    mix_copy = pltpu.make_async_copy(mixb, mix_hbm, mix_sem)
    mix_copy.start()
    arrived(stat.at[: nseq - 1], stat_r)
    peaks = stat[:, 0, :]
    top = jnp.max(peaks, axis=0, keepdims=True)
    whole = jnp.sum(jnp.exp(peaks - top) * stat[:, 1, :], axis=0, keepdims=True)
    near = []
    for h in range(2):
        u, v = place[h]
        for k in range(SIDE):
            near.append(stat[seq_of(h, before(SIDE, u, k), v), 0:1])
    near = jnp.exp(jnp.concatenate(near, axis=0) - top) / whole
    fac[...] = by_stream(jnp.concatenate([near] * (BLOCK // (2 * SIDE)), axis=0).T)
    for h in range(2):
        u, _ = place[h]
        mine = fac[pl.ds(pl.multiple_of(h * 2 * prow + (u // 2) * prow, prow), prow)]
        for k in range(SIDE):
            scales[h, k] = jnp.broadcast_to(
                mine[:, h * SIDE + k : h * SIDE + k + 1], (prow, BLOCK)
            )

    order = (
        (mid_sum, 0),
        (start_sum, 2),
        (mid_sum, 1),
        (end_sum, 0),
        (mid_sum, 2),
        (end_sum, 1),
        (mid_put, 0),
        (end_sum, 2),
        (mid_put, 1),
        (mid_put, 2),
        (end_put, 0),
        (end_put, 1),
        (end_put, 2),
    )

    for p in range(2):
        for step, s in order:
            if p == 0 and (step, s) == (end_put, 0):
                wg_copy.wait()
                wu_copy.wait()
                wd_copy.wait()
            for h in range(2):
                step(p, h, s)

    mix_copy.wait()

    arrived(stat.at[: nseq - 1], sent.at[0, 0])
    for p in range(2):
        arrived(first.at[p, :, :, : SIDE - 1], sent.at[1, p])
        arrived(second.at[p, :, :, : SIDE * ngrp - 1], sent.at[2, p])
        arrived(ys.at[:, :, :, :, : (SIDE - 1) * pw], sent.at[3, p])
        arrived(first.at[p, :, :, : SIDE - 1], sent.at[4, p])


def mix_kernel(mix_hbm, slots_hbm, out_hbm, mix, slots, out, mix_sem, in_sem, out_sem):
    parts, slot_count, tile = slots.shape
    mix_copy = pltpu.make_async_copy(mix_hbm, mix, mix_sem)
    mix_copy.start()

    def fetch(n):
        at = slice(n * tile, (n + 1) * tile)
        return pltpu.make_async_copy(slots_hbm.at[:, at], slots.at[n], in_sem.at[n])

    def store(n):
        at = slice(n * tile, (n + 1) * tile)
        return pltpu.make_async_copy(out.at[n % 4], out_hbm.at[:, at], out_sem.at[n % 4])

    for n in range(parts):
        fetch(n).start()
    mix_copy.wait()
    for n in range(parts):
        fetch(n).wait()
        if n >= 4:
            store(n - 4).wait()
        out[n % 4] = jnp.dot(mix[...], slots[n], preferred_element_type=F32).astype(BF16)
        store(n).start()
    for n in range(parts - 4, parts):
        store(n).wait()


def body(tokens, block_map, slot_keys, gate_weight, up_weight, down_weight):
    _, rows, width = tokens.shape
    slots = slot_keys.shape[1]
    nseq = lax.axis_size("seq")
    ngrp = lax.axis_size("grp")
    hidden = gate_weight.shape[2]
    cw = width // CHUNKS
    bw = cw // 2
    pw = bw // SIDE
    prow = slots // 4
    per = prow // ngrp
    anywhere = pl.BlockSpec(memory_space=pltpu.HBM)
    streams = (2, 2, CHUNKS)
    dma = pltpu.SemaphoreType.DMA
    mix, seq_slots = pl.pallas_call(
        functools.partial(layer_kernel, (nseq, ngrp, 3 * slots // 4)),
        out_shape=(
            pltpu.HBM((rows, slots), BF16),
            pltpu.HBM((ngrp, 2, 2, per, width), BF16),
        ),
        in_specs=[anywhere] * 6,
        out_specs=(anywhere, anywhere),
        scratch_shapes=[
            pltpu.VMEM((rows, width), BF16),
            pltpu.SMEM(block_map.shape, jnp.int32),
            pltpu.VMEM(slot_keys.shape, BF16),
            pltpu.VMEM(gate_weight.shape, BF16),
            pltpu.VMEM(up_weight.shape, BF16),
            pltpu.VMEM(down_weight.shape, BF16),
            pltpu.VMEM((rows, slots), F32),
            pltpu.VMEM((slots, rows), BF16),
            pltpu.VMEM((rows, slots), BF16),
            pltpu.VMEM((slots, BLOCK), F32),
            pltpu.VMEM((2, SIDE, prow, BLOCK), F32),
            pltpu.VMEM((nseq, 2, slots), F32),
            pltpu.VMEM((2, 2, 2, prow, width), BF16),
            pltpu.VMEM((*streams, SIDE, prow, bw), BF16),
            pltpu.VMEM((*streams, ngrp, per, bw), BF16),
            pltpu.VMEM((*streams, SIDE * ngrp, per, pw), BF16),
            pltpu.VMEM((2, 2, prow, width), BF16),
            pltpu.VMEM((2, 2 * prow, hidden), F32),
            pltpu.VMEM((2, 2 * prow, hidden), F32),
            pltpu.VMEM((2, CHUNKS, ngrp, per, bw), BF16),
            dma((4,)),
            dma((5,)),
            dma,
            dma((2, CHUNKS)),
            dma((5, 2)),
            dma,
            dma(streams),
            dma(streams),
            dma(streams),
            dma(streams),
        ],
        compiler_params=pltpu.CompilerParams(
            collective_id=0, has_side_effects=True, vmem_limit_bytes=63 << 20
        ),
    )(
        tokens,
        pltpu.with_memory_space_constraint(block_map, pltpu.HBM),
        pltpu.with_memory_space_constraint(slot_keys, pltpu.HBM),
        gate_weight,
        up_weight,
        down_weight,
    )

    tile = width // 6
    out = pl.pallas_call(
        mix_kernel,
        out_shape=jax.ShapeDtypeStruct((rows, width), BF16),
        in_specs=[anywhere] * 2,
        out_specs=anywhere,
        scratch_shapes=[
            pltpu.VMEM((rows, slots), BF16),
            pltpu.VMEM((6, slots, tile), BF16),
            pltpu.VMEM((4, rows, tile), BF16),
            dma,
            dma((6,)),
            dma((4,)),
        ],
        compiler_params=pltpu.CompilerParams(vmem_limit_bytes=60 << 20),
    )(mix, seq_slots.reshape(slots, width))
    return out[None]


def solution(mesh):
    placed = (
        P("grp", "seq", None),
        P("grp", "seq"),
        P(),
        P("grp", None, "seq"),
        P("grp", None, "seq"),
        P("grp", "seq", None),
    )
    return jax.shard_map(
        body, mesh=mesh, in_specs=placed, out_specs=P("grp", "seq", None), check_vma=False
    )
```

time: 92.5 us -> 73.2 us (0.79)
  Pallas kernels: 90.9 us -> 72.7 us
  local copies, waits for them, and re-layouts: 1.45 us -> 0 us
    pallas_call x1, Pallas kernels: 85 us -> 67.6 us  [body(): pl.pallas_call(functools.partial(layer_kernel, (nseq, ngrp, 3 * slots //...]
    unnamed x4 -> x0, local copies, waits for them, and re-layouts: 1.45 us -> none
where the time goes in v3:
time: 73.2 us; the launch traced here: 72.7 us
  Pallas kernels  72.7 us (99%)
    pallas_call x1, Pallas kernels, body(): pl.pallas_call(functools.partial(layer_kernel, (nseq, ngrp, 3 * slots //...  67.6 us
    pallas_call x1, Pallas kernels, body(): pl.pallas_call(mix_kernel, out_shape=jax.ShapeDtypeStruct((rows, width),...  5.12 us

profile of v3, /device:TPU:0, one launch (start us, length us, event | category | flops | bytes accessed | tf_op | source)
XLA Modules:
  0.0 72.7 jit_solution(11041485334851836792)
XLA Ops:
  0.0 67.6 %shard_map.64 = (bf16[1024,256]{1,0:T(8,128)(2,1)}, bf16[8,2,2,8,3072]{4,3,2,1,0:T(8,128)(2,1)}) custom-call(bf16[1,1024,3072]{2,1,0:T(8,128)(2,1)} %tok_hbm.1, s32[1,8]{1,0:T(1,128)} %bm_hbm.1, bf16[3072,256]{1,0:T(8,128)(2,1)} %keys_hbm.1, bf16[2,3072,256]{2,1,0:T(8,128)(2,1)} %wg_hbm.1, bf16[2,3072,256]{2,1,0:T(8,128)(2,1)} %wu_hbm.1, ...), custom_call_target="tpu_custom_call" | custom-call | tf_op jit(solution)/shard_map/pallas_call | solution.py:437
  67.6 5.1 %shard_map.65 = bf16[1024,3072]{1,0:T(8,128)(2,1)} custom-call(bf16[1024,256]{1,0:T(8,128)(2,1)} %get-tuple-element.7.mix_hbm, bf16[256,3072]{1,0:T(8,128)(2,1)} %bitcast.2), custom_call_target="tpu_custom_call" | custom-call | tf_op jit(solution)/shard_map/pallas_call | solution.py:490

commit v4 on v3

--- a/solution.py
+++ b/solution.py
@@ -20,6 +20,13 @@
         return carry
 
     lax.fori_loop(start, stop, step, 0)
+
+
+def far_first(n, m):
+    def hops(k):
+        return min(k // m, n - k // m) + min(k % m, m - k % m)
+
+    return sorted(range(1, n * m), key=hops, reverse=True)
 
 
 def layer_kernel(
@@ -48,6 +55,9 @@
     first,
     middle,
     second,
+    piece_x,
+    piece_y,
+    counts,
     xs,
     gates,
     ups,
@@ -62,10 +72,13 @@
     sum_lr,
     put_lr,
     put_hr,
+    pass_hr,
 ):
     nseq, ngrp, image_slots = dims
     me = lax.axis_index("seq")
     grp = lax.axis_index("grp")
+    level, core = grp // 2, lax.rem(grp, 2)
+    levels = ngrp // 2
     rows, width = tok.shape
     slots = keys.shape[1]
     tchunk = rows // 4
@@ -74,6 +87,7 @@
     bw = cw // 2
     pw = bw // SIDE
     prow = slots // 4
+    per_grp = prow // ngrp
     at_x, at_y = me // SIDE, lax.rem(me, SIDE)
     place = ((at_x, at_y), (at_y, at_x))
 
@@ -112,10 +126,19 @@
         u, v = place[h]
 
         def greet_line(k):
-            peer = seq_of(h, u, lax.rem(v + k // ngrp, SIDE))
-            greet({"seq": peer, "grp": lax.rem(grp + k, ngrp)})
-
-        loop(ngrp if h else 1, SIDE * ngrp, greet_line)
+            peer = seq_of(h, u, lax.rem(v + k, SIDE))
+            greet({"seq": peer, "grp": level * 2 + 1 - core})
+
+            def greet_level(n):
+                greet({"seq": peer, "grp": lax.rem(level + n, levels) * 2 + core})
+
+            loop(1, levels, greet_level)
+
+        def greet_near(k):
+            greet({"seq": seq_of(h, u, lax.rem(v + k, SIDE))})
+
+        loop(h, SIDE, greet_line)
+        loop(1, SIDE, greet_near)
 
     def greet_rest(k):
         x = lax.rem(at_x + 1 + k // (SIDE - 1), SIDE)
@@ -123,7 +146,7 @@
         greet({"seq": x * SIDE + y})
 
     loop(0, (SIDE - 1) * (SIDE - 1), greet_rest)
-    greeted = (2 * SIDE - 1) * ngrp - 1 + (SIDE - 1) * (SIDE - 1)
+    greeted = (2 * SIDE - 1) * levels + nseq - 1
 
     def to(src, dst, ssem, rsem, peer, **more):
         return pltpu.make_async_remote_copy(
@@ -203,31 +226,33 @@
             seq_of(h, dst, v),
         )
 
-    def sum_light(p, h, s, dst, dst_grp, src, src_grp):
+    def sum_light(p, h, s, dst, dst_core, src, src_core):
         u, _ = place[h]
         return to(
-            middle.at[p, h, s, dst_grp, :, piece_at(dst)],
-            second.at[p, h, s, src * ngrp + src_grp],
+            middle.at[p, h, s, :, dst_core, :, piece_at(dst)],
+            second.at[p, h, s, src * 2 + src_core],
             sent.at[2, p],
             sum_lr.at[p, h, s],
             seq_of(h, u, dst),
-            grp=dst_grp,
-        )
-
-    def put_light(p, h, s, dst, src):
-        u, v = place[h]
+            grp=level * 2 + dst_core,
+        )
+
+    def put_light(p, h, s, dst, dst_level, src, src_level):
+        u, _ = place[h]
         if p == 0:
-            here = xs.at[h, u // 2, :, piece_cols(s, u, v)]
-            there = xs.at[h, u // 2, :, piece_cols(s, u, src)]
+            here = piece_x.at[h, s, dst_level]
+            at = pl.ds(pl.multiple_of(src_level * 2 * per_grp, 2 * per_grp), 2 * per_grp)
+            there = xs.at[h, u // 2, at, piece_cols(s, u, src)]
         else:
-            here = ys.at[h, s, :, :, piece_at(v)]
-            there = ys.at[h, s, :, :, piece_at(src)]
+            here = piece_y.at[h, s, dst_level]
+            there = ys.at[h, s, src_level, :, :, piece_at(src)]
         return to(
             here,
             there,
             sent.at[3, p],
             put_lr.at[p, h, s],
             seq_of(h, u, dst),
+            grp=dst_level * 2 + core,
         )
 
     def put_heavy(p, h, s, dst, src):
@@ -237,7 +262,7 @@
             there = xs.at[h, src // 2, :, block_cols(s, src)]
         else:
             here = ys.at[h, s]
-            there = slots_hbm.at[:, h, src // 2, :, block_cols(s, src)]
+            there = slots_hbm.at[:, :, h, src // 2, :, block_cols(s, src)]
         return to(
             here,
             there,
@@ -246,10 +271,24 @@
             seq_of(h, dst, v),
         )
 
+    def pass_half(p, h, s, side):
+        u, v = place[h]
+        step = (1, SIDE - 1)[side]
+        src, dst = before(SIDE, u, step), around(SIDE, u, step)
+        if p == 0:
+            rows_of = slice(side * prow // 2, (side + 1) * prow // 2)
+            half = xs.at[h, src // 2, rows_of, block_cols(s, src)]
+        else:
+            levels_of = slice(side * levels // 2, (side + 1) * levels // 2)
+            half = slots_hbm.at[levels_of, :, h, src // 2, :, block_cols(s, src)]
+        return to(half, half, sent.at[4, p], pass_hr.at[p, h, s], seq_of(h, dst, v))
+
     def own_copy(h, s):
         u, _ = place[h]
         return pltpu.make_async_copy(
-            ys.at[h, s], slots_hbm.at[:, h, u // 2, :, block_cols(s, u)], own_sem.at[h, s]
+            ys.at[h, s],
+            slots_hbm.at[:, :, h, u // 2, :, block_cols(s, u)],
+            own_sem.at[h, s],
         )
 
     def start_sum(p, h, s):
@@ -271,37 +310,59 @@
         middle[p, h, s] = acc.reshape(middle.shape[3:]).astype(BF16)
 
         def send(k):
-            dst, dst_grp = around(SIDE, v, k // ngrp), around(ngrp, grp, k)
-            sum_light(p, h, s, dst, dst_grp, v, grp).start()
-
-        loop(1, SIDE * ngrp, send)
-        second[p, h, s, v * ngrp + grp] = middle[p, h, s, grp, :, piece_at(v)]
+            dst, dst_core = around(SIDE, v, k // 2), lax.rem(core + k, 2)
+            sum_light(p, h, s, dst, dst_core, v, core).start()
+
+        for k in far_first(SIDE, 2):
+            send(k)
+        second[p, h, s, v * 2 + core] = middle[p, h, s, :, core, :, piece_at(v)]
 
     def scale_of(h, k):
         return jnp.concatenate([scales[h, k]] * (bw // BLOCK), axis=1)
 
     def end_sum(p, h, s):
         u, v = place[h]
-        arrived(second.at[p, h, s, : SIDE * ngrp - 1], sum_lr.at[p, h, s])
-        acc = second[p, h, s, :ngrp].astype(F32)
-        for k in range(1, SIDE):
-            acc = acc + second[p, h, s, k * ngrp : (k + 1) * ngrp].astype(F32)
+        arrived(second.at[p, h, s, : SIDE * 2 - 1], sum_lr.at[p, h, s])
+        for c in range(2):
+            acc = second[p, h, s, c].astype(F32)
+            for k in range(1, SIDE):
+                acc = acc + second[p, h, s, 2 * k + c].astype(F32)
+            if p == 0:
+                piece_x[h, s, :, c * per_grp : (c + 1) * per_grp] = acc.astype(BF16)
+            else:
+                piece_y[h, s, :, c] = acc.astype(BF16)
+
+        def send(k):
+            dst, dst_level = around(SIDE, v, k // levels), around(levels, level, lax.rem(k, levels))
+            put_light(p, h, s, dst, dst_level, v, level).start()
+
+        for k in far_first(SIDE, levels):
+            send(k)
         if p == 0:
-            piece = acc.reshape(prow, pw).astype(BF16)
-            xs[h, u // 2, :, piece_cols(s, u, v)] = piece
+            at = pl.ds(pl.multiple_of(level * 2 * per_grp, 2 * per_grp), 2 * per_grp)
+            xs[h, u // 2, at, piece_cols(s, u, v)] = piece_x[h, s, level]
         else:
-            ys[h, s, :, :, piece_at(v)] = acc.astype(BF16)
-        loop(1, SIDE, lambda k: put_light(p, h, s, around(SIDE, v, k), v).start())
+            ys[h, s, level, :, :, piece_at(v)] = piece_y[h, s, level]
 
     def mid_put(p, h, s):
         u, v = place[h]
-        arrived(ys.at[h, s, :, :, : (SIDE - 1) * pw], put_lr.at[p, h, s])
-        loop(1, SIDE, lambda k: put_heavy(p, h, s, around(SIDE, u, k), u).start())
+        arrived(counts.at[0, : SIDE * levels - 1], put_lr.at[p, h, s])
+        u, _ = place[h]
+        for k in (1, 2, 3) if s == CHUNKS - 1 else (1, 3):
+            put_heavy(p, h, s, around(SIDE, u, k), u).start()
         if p == 1:
             own_copy(h, s).start()
 
+    def pass_put(p, h, s):
+        arrived(first.at[p, h, s, :2], put_hr.at[p, h, s])
+        for side in range(2):
+            pass_half(p, h, s, side).start()
+
     def end_put(p, h, s):
-        arrived(first.at[p, h, s, : SIDE - 1], put_hr.at[p, h, s])
+        if s < CHUNKS - 1:
+            arrived(first.at[p, h, s, 0], pass_hr.at[p, h, s])
+        else:
+            arrived(first.at[p, h, s, : SIDE - 1], put_hr.at[p, h, s])
         if p == 1:
             own_copy(h, s).wait()
             return
@@ -320,7 +381,7 @@
             at = slice(n * cw, (n + 1) * cw)
             out = jnp.dot(hidden, wd[h, :, at], preferred_element_type=F32)
             terms[1, h, :, :, at] = out.reshape(2, prow, cw).astype(BF16)
-            if n < CHUNKS - 1:
+            if n < 2:
                 start_sum(1, h, n)
 
     def mix_rows(b):
@@ -333,7 +394,7 @@
         at = slice(s * cw, (s + 1) * cw)
         out = jnp.dot(wts[...], tok[:, at], preferred_element_type=F32)
         terms[0, :, :, :, at] = out.reshape(2, 2, prow, cw).astype(BF16)
-        if s < CHUNKS - 1:
+        if s < 2:
             for h in range(2):
                 start_sum(0, h, s)
 
@@ -369,7 +430,9 @@
         (mid_put, 0),
         (end_sum, 2),
         (mid_put, 1),
+        (pass_put, 0),
         (mid_put, 2),
+        (pass_put, 1),
         (end_put, 0),
         (end_put, 1),
         (end_put, 2),
@@ -389,8 +452,8 @@
     arrived(stat.at[: nseq - 1], sent.at[0, 0])
     for p in range(2):
         arrived(first.at[p, :, :, : SIDE - 1], sent.at[1, p])
-        arrived(second.at[p, :, :, : SIDE * ngrp - 1], sent.at[2, p])
-        arrived(ys.at[:, :, :, :, : (SIDE - 1) * pw], sent.at[3, p])
+        arrived(second.at[p, :, :, : SIDE * 2 - 1], sent.at[2, p])
+        arrived(counts.at[:, : SIDE * levels - 1], sent.at[3, p])
         arrived(first.at[p, :, :, : SIDE - 1], sent.at[4, p])
 
 
@@ -438,7 +501,7 @@
         functools.partial(layer_kernel, (nseq, ngrp, 3 * slots // 4)),
         out_shape=(
             pltpu.HBM((rows, slots), BF16),
-            pltpu.HBM((ngrp, 2, 2, per, width), BF16),
+            pltpu.HBM((ngrp // 2, 2, 2, 2, per, width), BF16),
         ),
         in_specs=[anywhere] * 6,
         out_specs=(anywhere, anywhere),
@@ -457,18 +520,22 @@
             pltpu.VMEM((nseq, 2, slots), F32),
             pltpu.VMEM((2, 2, 2, prow, width), BF16),
             pltpu.VMEM((*streams, SIDE, prow, bw), BF16),
-            pltpu.VMEM((*streams, ngrp, per, bw), BF16),
-            pltpu.VMEM((*streams, SIDE * ngrp, per, pw), BF16),
+            pltpu.VMEM((*streams, ngrp // 2, 2, per, bw), BF16),
+            pltpu.VMEM((*streams, SIDE * 2, ngrp // 2, per, pw), BF16),
+            pltpu.VMEM((2, CHUNKS, ngrp // 2, 2 * per, pw), BF16),
+            pltpu.VMEM((2, CHUNKS, ngrp // 2, 2, per, pw), BF16),
+            pltpu.VMEM((2 * CHUNKS, SIDE * ngrp // 2, 2 * per, pw), BF16),
             pltpu.VMEM((2, 2, prow, width), BF16),
             pltpu.VMEM((2, 2 * prow, hidden), F32),
             pltpu.VMEM((2, 2 * prow, hidden), F32),
-            pltpu.VMEM((2, CHUNKS, ngrp, per, bw), BF16),
+            pltpu.VMEM((2, CHUNKS, ngrp // 2, 2, per, bw), BF16),
             dma((4,)),
             dma((5,)),
             dma,
             dma((2, CHUNKS)),
             dma((5, 2)),
             dma,
+            dma(streams),
             dma(streams),
             dma(streams),
             dma(streams),

time: 73.2 us -> 70.5 us (0.963)
  Pallas kernels: 72.7 us -> 70.4 us
    pallas_call x1, Pallas kernels: 67.6 us -> 65.3 us  [body(): pl.pallas_call(functools.partial(layer_kernel, (nseq, ngrp, 3 * slots //...]
where the time goes in v4:
time: 70.5 us; the launch traced here: 70.4 us
  Pallas kernels  70.4 us (100%)
    pallas_call x1, Pallas kernels, body(): pl.pallas_call(functools.partial(layer_kernel, (nseq, ngrp, 3 * slots //...  65.3 us
    pallas_call x1, Pallas kernels, body(): pl.pallas_call(mix_kernel, out_shape=jax.ShapeDtypeStruct((rows, width),...  5.12 us

profile of v4, /device:TPU:0, one launch (start us, length us, event | category | flops | bytes accessed | tf_op | source)
XLA Modules:
  0.0 70.4 jit_solution(13189947955710401950)
XLA Ops:
  0.0 65.3 %shard_map.64 = (bf16[1024,256]{1,0:T(8,128)(2,1)}, bf16[4,2,2,2,8,3072]{5,4,3,2,1,0:T(8,128)(2,1)}) custom-call(bf16[1,1024,3072]{2,1,0:T(8,128)(2,1)} %tok_hbm.1, s32[1,8]{1,0:T(1,128)} %bm_hbm.1, bf16[3072,256]{1,0:T(8,128)(2,1)} %keys_hbm.1, bf16[2,3072,256]{2,1,0:T(8,128)(2,1)} %wg_hbm.1, bf16[2,3072,256]{2,1,0:T(8,128)(2,1)} %wu_hbm.1, ...), custom_call_target="tpu_custom_call" | custom-call | tf_op jit(solution)/shard_map/pallas_call | solution.py:500
  65.3 5.1 %shard_map.65 = bf16[1024,3072]{1,0:T(8,128)(2,1)} custom-call(bf16[1024,256]{1,0:T(8,128)(2,1)} %get-tuple-element.7.mix_hbm, bf16[256,3072]{1,0:T(8,128)(2,1)} %bitcast.2), custom_call_target="tpu_custom_call" | custom-call | tf_op jit(solution)/shard_map/pallas_call | solution.py:557

commit v5 on v4

--- a/solution.py
+++ b/solution.py
@@ -37,8 +37,8 @@
     wg_hbm,
     wu_hbm,
     wd_hbm,
-    mix_hbm,
-    slots_hbm,
+    mix_out,
+    slots_out,
     tok,
     bm,
     keys,
@@ -47,7 +47,6 @@
     wd,
     logits,
     wts,
-    mixb,
     fac,
     scales,
     stat,
@@ -64,7 +63,6 @@
     ys,
     tok_sem,
     in_sem,
-    mix_sem,
     own_sem,
     sent,
     stat_r,
@@ -262,7 +260,7 @@
             there = xs.at[h, src // 2, :, block_cols(s, src)]
         else:
             here = ys.at[h, s]
-            there = slots_hbm.at[:, :, h, src // 2, :, block_cols(s, src)]
+            there = slots_out.at[:, :, h, src // 2, :, block_cols(s, src)]
         return to(
             here,
             there,
@@ -280,14 +278,14 @@
             half = xs.at[h, src // 2, rows_of, block_cols(s, src)]
         else:
             levels_of = slice(side * levels // 2, (side + 1) * levels // 2)
-            half = slots_hbm.at[levels_of, :, h, src // 2, :, block_cols(s, src)]
+            half = slots_out.at[levels_of, :, h, src // 2, :, block_cols(s, src)]
         return to(half, half, sent.at[4, p], pass_hr.at[p, h, s], seq_of(h, dst, v))
 
     def own_copy(h, s):
         u, _ = place[h]
         return pltpu.make_async_copy(
             ys.at[h, s],
-            slots_hbm.at[:, :, h, u // 2, :, block_cols(s, u)],
+            slots_out.at[:, :, h, u // 2, :, block_cols(s, u)],
             own_sem.at[h, s],
         )
 
@@ -388,7 +386,7 @@
         at = pl.ds(pl.multiple_of(b * BLOCK, BLOCK), BLOCK)
         m = logits[at]
         e = jnp.where(text_lane == bm[0, b], jnp.exp(m - jnp.max(m, axis=1, keepdims=True)), 0.0)
-        mixb[at] = (e / jnp.sum(e, axis=1, keepdims=True)).astype(BF16)
+        mix_out[at] = (e / jnp.sum(e, axis=1, keepdims=True)).astype(BF16)
 
     for s in range(CHUNKS):
         at = slice(s * cw, (s + 1) * cw)
@@ -399,8 +397,6 @@
                 start_sum(0, h, s)
 
     loop(0, blocks, mix_rows)
-    mix_copy = pltpu.make_async_copy(mixb, mix_hbm, mix_sem)
-    mix_copy.start()
     arrived(stat.at[: nseq - 1], stat_r)
     peaks = stat[:, 0, :]
     top = jnp.max(peaks, axis=0, keepdims=True)
@@ -447,7 +443,6 @@
             for h in range(2):
                 step(p, h, s)
 
-    mix_copy.wait()
 
     arrived(stat.at[: nseq - 1], sent.at[0, 0])
     for p in range(2):
@@ -457,27 +452,20 @@
         arrived(first.at[p, :, :, : SIDE - 1], sent.at[4, p])
 
 
-def mix_kernel(mix_hbm, slots_hbm, out_hbm, mix, slots, out, mix_sem, in_sem, out_sem):
-    parts, slot_count, tile = slots.shape
-    mix_copy = pltpu.make_async_copy(mix_hbm, mix, mix_sem)
-    mix_copy.start()
-
-    def fetch(n):
-        at = slice(n * tile, (n + 1) * tile)
-        return pltpu.make_async_copy(slots_hbm.at[:, at], slots.at[n], in_sem.at[n])
+def mix_kernel(mix, slots, out_hbm, out, out_sem):
+    tile = out.shape[2]
+    parts = slots.shape[1] // tile
 
     def store(n):
         at = slice(n * tile, (n + 1) * tile)
         return pltpu.make_async_copy(out.at[n % 4], out_hbm.at[:, at], out_sem.at[n % 4])
 
     for n in range(parts):
-        fetch(n).start()
-    mix_copy.wait()
-    for n in range(parts):
-        fetch(n).wait()
         if n >= 4:
             store(n - 4).wait()
-        out[n % 4] = jnp.dot(mix[...], slots[n], preferred_element_type=F32).astype(BF16)
+        out[n % 4] = jnp.dot(
+            mix[...], slots[:, n * tile : (n + 1) * tile], preferred_element_type=F32
+        ).astype(BF16)
         store(n).start()
     for n in range(parts - 4, parts):
         store(n).wait()
@@ -495,16 +483,17 @@
     prow = slots // 4
     per = prow // ngrp
     anywhere = pl.BlockSpec(memory_space=pltpu.HBM)
+    on_chip = pl.BlockSpec(memory_space=pltpu.VMEM)
     streams = (2, 2, CHUNKS)
     dma = pltpu.SemaphoreType.DMA
     mix, seq_slots = pl.pallas_call(
         functools.partial(layer_kernel, (nseq, ngrp, 3 * slots // 4)),
         out_shape=(
-            pltpu.HBM((rows, slots), BF16),
-            pltpu.HBM((ngrp // 2, 2, 2, 2, per, width), BF16),
+            pltpu.VMEM((rows, slots), BF16),
+            pltpu.VMEM((ngrp // 2, 2, 2, 2, per, width), BF16),
         ),
         in_specs=[anywhere] * 6,
-        out_specs=(anywhere, anywhere),
+        out_specs=(on_chip, on_chip),
         scratch_shapes=[
             pltpu.VMEM((rows, width), BF16),
             pltpu.SMEM(block_map.shape, jnp.int32),
@@ -514,7 +503,6 @@
             pltpu.VMEM(down_weight.shape, BF16),
             pltpu.VMEM((rows, slots), F32),
             pltpu.VMEM((slots, rows), BF16),
-            pltpu.VMEM((rows, slots), BF16),
             pltpu.VMEM((slots, BLOCK), F32),
             pltpu.VMEM((2, SIDE, prow, BLOCK), F32),
             pltpu.VMEM((nseq, 2, slots), F32),
@@ -531,7 +519,6 @@
             pltpu.VMEM((2, CHUNKS, ngrp // 2, 2, per, bw), BF16),
             dma((4,)),
             dma((5,)),
-            dma,
             dma((2, CHUNKS)),
             dma((5, 2)),
             dma,
@@ -542,32 +529,23 @@
             dma(streams),
         ],
         compiler_params=pltpu.CompilerParams(
-            collective_id=0, has_side_effects=True, vmem_limit_bytes=63 << 20
+            collective_id=0, has_side_effects=True, vmem_limit_bytes=56 << 20
         ),
     )(
-        tokens,
-        pltpu.with_memory_space_constraint(block_map, pltpu.HBM),
-        pltpu.with_memory_space_constraint(slot_keys, pltpu.HBM),
-        gate_weight,
-        up_weight,
-        down_weight,
+        *(
+            pltpu.with_memory_space_constraint(x, pltpu.HBM)
+            for x in (tokens, block_map, slot_keys, gate_weight, up_weight, down_weight)
+        )
     )
 
     tile = width // 6
     out = pl.pallas_call(
         mix_kernel,
         out_shape=jax.ShapeDtypeStruct((rows, width), BF16),
-        in_specs=[anywhere] * 2,
+        in_specs=[on_chip] * 2,
         out_specs=anywhere,
-        scratch_shapes=[
-            pltpu.VMEM((rows, slots), BF16),
-            pltpu.VMEM((6, slots, tile), BF16),
-            pltpu.VMEM((4, rows, tile), BF16),
-            dma,
-            dma((6,)),
-            dma((4,)),
-        ],
-        compiler_params=pltpu.CompilerParams(vmem_limit_bytes=60 << 20),
+        scratch_shapes=[pltpu.VMEM((4, rows, tile), BF16), dma((4,))],
+        compiler_params=pltpu.CompilerParams(vmem_limit_bytes=32 << 20),
     )(mix, seq_slots.reshape(slots, width))
     return out[None]
 

time: 70.5 us -> 68.3 us (0.969)
  Pallas kernels: 70.4 us -> 68.1 us
    pallas_call x1, Pallas kernels: 5.12 us -> 3.28 us  [body(): pl.pallas_call(mix_kernel, out_shape=jax.ShapeDtypeStruct((rows, width),...]
where the time goes in v5:
time: 68.3 us; the launch traced here: 68.2 us
  Pallas kernels  68.1 us (100%)
    pallas_call x1, Pallas kernels, body(): pl.pallas_call(functools.partial(layer_kernel, (nseq, ngrp, 3 * slots //...  64.9 us
    pallas_call x1, Pallas kernels, body(): pl.pallas_call(mix_kernel, out_shape=jax.ShapeDtypeStruct((rows, width),...  3.28 us

profile of v5, /device:TPU:0, one launch (start us, length us, event | category | flops | bytes accessed | tf_op | source)
XLA Modules:
  0.0 68.2 jit_solution(1717923615626140166)
XLA Ops:
  0.0 64.9 %shard_map.64 = (bf16[1024,256]{1,0:T(8,128)(2,1)S(1)}, bf16[4,2,2,2,8,3072]{5,4,3,2,1,0:T(8,128)(2,1)S(1)}) custom-call(bf16[1,1024,3072]{2,1,0:T(8,128)(2,1)} %tok_hbm.1, s32[1,8]{1,0:T(1,128)} %bm_hbm.1, bf16[3072,256]{1,0:T(8,128)(2,1)} %keys_hbm.1, bf16[2,3072,256]{2,1,0:T(8,128)(2,1)} %wg_hbm.1, bf16[2,3072,256]{2,1,0:T(8,128)(2,1)} %wu_hbm.1, ...), custom_call_target="tpu_custom_call" | custom-call | tf_op jit(solution)/shard_map/pallas_call | solution.py:489
  64.9 3.3 %shard_map.65 = bf16[1024,3072]{1,0:T(8,128)(2,1)} custom-call(bf16[1024,256]{1,0:T(8,128)(2,1)S(1)} %get-tuple-element.7.mix, bf16[256,3072]{1,0:T(8,128)(2,1)S(1)} %bitcast.2), custom_call_target="tpu_custom_call" | custom-call | tf_op jit(solution)/shard_map/pallas_call | solution.py:542

commit v6 on v5

--- a/solution.py
+++ b/solution.py
@@ -374,13 +374,16 @@
             gates[h] = gate
             ups[h] = up
             return
-        hidden = (gate / (1.0 + jnp.exp(-gate)) * up).astype(BF16)
+        gates[h] = gate / (1.0 + jnp.exp(-gate)) * up
+        if h == 0:
+            return
         for n in range(CHUNKS):
-            at = slice(n * cw, (n + 1) * cw)
-            out = jnp.dot(hidden, wd[h, :, at], preferred_element_type=F32)
-            terms[1, h, :, :, at] = out.reshape(2, prow, cw).astype(BF16)
-            if n < 2:
-                start_sum(1, h, n)
+            for e in range(2):
+                at = slice(n * cw, (n + 1) * cw)
+                out = jnp.dot(gates[e].astype(BF16), wd[e, :, at], preferred_element_type=F32)
+                terms[1, e, :, :, at] = out.reshape(2, prow, cw).astype(BF16)
+                if n < 2:
+                    start_sum(1, e, n)
 
     def mix_rows(b):
         at = pl.ds(pl.multiple_of(b * BLOCK, BLOCK), BLOCK)

time: 68.3 us -> 67.6 us (0.990)
  no operation moved by 1% of the time
where the time goes in v6:
time: 67.6 us; the launch traced here: 67.5 us
  Pallas kernels  67.5 us (100%)
    pallas_call x1, Pallas kernels, body(): pl.pallas_call(functools.partial(layer_kernel, (nseq, ngrp, 3 * slots //...  64.2 us
    pallas_call x1, Pallas kernels, body(): pl.pallas_call(mix_kernel, out_shape=jax.ShapeDtypeStruct((rows, width),...  3.28 us

profile of v6, /device:TPU:0, one launch (start us, length us, event | category | flops | bytes accessed | tf_op | source)
XLA Modules:
  0.0 67.5 jit_solution(5338044394573908465)
XLA Ops:
  0.0 64.2 %shard_map.64 = (bf16[1024,256]{1,0:T(8,128)(2,1)S(1)}, bf16[4,2,2,2,8,3072]{5,4,3,2,1,0:T(8,128)(2,1)S(1)}) custom-call(bf16[1,1024,3072]{2,1,0:T(8,128)(2,1)} %tok_hbm.1, s32[1,8]{1,0:T(1,128)} %bm_hbm.1, bf16[3072,256]{1,0:T(8,128)(2,1)} %keys_hbm.1, bf16[2,3072,256]{2,1,0:T(8,128)(2,1)} %wg_hbm.1, bf16[2,3072,256]{2,1,0:T(8,128)(2,1)} %wu_hbm.1, ...), custom_call_target="tpu_custom_call" | custom-call | tf_op jit(solution)/shard_map/pallas_call | solution.py:492
  64.3 3.3 %shard_map.65 = bf16[1024,3072]{1,0:T(8,128)(2,1)} custom-call(bf16[1024,256]{1,0:T(8,128)(2,1)S(1)} %get-tuple-element.7.mix, bf16[256,3072]{1,0:T(8,128)(2,1)S(1)} %bitcast.2), custom_call_target="tpu_custom_call" | custom-call | tf_op jit(solution)/shard_map/pallas_call | solution.py:545

commit v7 on v6

--- a/solution.py
+++ b/solution.py
@@ -110,7 +110,7 @@
         at = pl.ds(pl.multiple_of(r * tchunk, tchunk), tchunk)
         return pltpu.make_async_copy(tok_hbm.at[0, at], tok.at[at], tok_sem.at[r])
 
-    loop(0, 4, lambda r: tok_copy(r).start())
+    tok_copy(0).start()
     wg_copy = pltpu.make_async_copy(wg_hbm, wg, in_sem.at[1])
     wu_copy = pltpu.make_async_copy(wu_hbm, wu, in_sem.at[2])
     wd_copy = pltpu.make_async_copy(wd_hbm, wd, in_sem.at[3])
@@ -144,6 +144,7 @@
         greet({"seq": x * SIDE + y})
 
     loop(0, (SIDE - 1) * (SIDE - 1), greet_rest)
+    loop(1, 4, lambda r: tok_copy(r).start())
     greeted = (2 * SIDE - 1) * levels + nseq - 1
 
     def to(src, dst, ssem, rsem, peer, **more):
@@ -346,7 +347,7 @@
         u, v = place[h]
         arrived(counts.at[0, : SIDE * levels - 1], put_lr.at[p, h, s])
         u, _ = place[h]
-        for k in (1, 2, 3) if s == CHUNKS - 1 else (1, 3):
+        for k in (1, 2, 3) if s >= 1 else (1, 3):
             put_heavy(p, h, s, around(SIDE, u, k), u).start()
         if p == 1:
             own_copy(h, s).start()
@@ -357,7 +358,7 @@
             pass_half(p, h, s, side).start()
 
     def end_put(p, h, s):
-        if s < CHUNKS - 1:
+        if s < 1:
             arrived(first.at[p, h, s, 0], pass_hr.at[p, h, s])
         else:
             arrived(first.at[p, h, s, : SIDE - 1], put_hr.at[p, h, s])
@@ -431,7 +432,6 @@
         (mid_put, 1),
         (pass_put, 0),
         (mid_put, 2),
-        (pass_put, 1),
         (end_put, 0),
         (end_put, 1),
         (end_put, 2),

time: 67.6 us -> 67.6 us (level)
  no operation moved by 1% of the time
where the time goes in v7:
time: 67.6 us; the launch traced here: 67.4 us
  Pallas kernels  67.4 us (100%)
    pallas_call x1, Pallas kernels, body(): pl.pallas_call(functools.partial(layer_kernel, (nseq, ngrp, 3 * slots //...  64.1 us
    pallas_call x1, Pallas kernels, body(): pl.pallas_call(mix_kernel, out_shape=jax.ShapeDtypeStruct((rows, width),...  3.28 us

profile of v7, /device:TPU:0, one launch (start us, length us, event | category | flops | bytes accessed | tf_op | source)
XLA Modules:
  0.0 67.4 jit_solution(3547369498008763795)
XLA Ops:
  0.0 64.1 %shard_map.64 = (bf16[1024,256]{1,0:T(8,128)(2,1)S(1)}, bf16[4,2,2,2,8,3072]{5,4,3,2,1,0:T(8,128)(2,1)S(1)}) custom-call(bf16[1,1024,3072]{2,1,0:T(8,128)(2,1)} %tok_hbm.1, s32[1,8]{1,0:T(1,128)} %bm_hbm.1, bf16[3072,256]{1,0:T(8,128)(2,1)} %keys_hbm.1, bf16[2,3072,256]{2,1,0:T(8,128)(2,1)} %wg_hbm.1, bf16[2,3072,256]{2,1,0:T(8,128)(2,1)} %wu_hbm.1, ...), custom_call_target="tpu_custom_call" | custom-call | tf_op jit(solution)/shard_map/pallas_call | solution.py:492
  64.1 3.3 %shard_map.65 = bf16[1024,3072]{1,0:T(8,128)(2,1)} custom-call(bf16[1024,256]{1,0:T(8,128)(2,1)S(1)} %get-tuple-element.7.mix, bf16[256,3072]{1,0:T(8,128)(2,1)S(1)} %bitcast.2), custom_call_target="tpu_custom_call" | custom-call | tf_op jit(solution)/shard_map/pallas_call | solution.py:545
